TPU v7x, 32 devices: a whole 2x2x4 slice. The times are simulated.
32 devices in a mesh: dp: 8 (over z, y), tensor: 4 (over x, core).
Axes of the slice: x: 2, y: 2, z: 4, core: 2. Of those that a mesh axis runs over, the one named last changes fastest.
Arguments:
- tokens: bfloat16 [4096, 768], P(('dp', 'tensor')), may hold values from -6 to 6
- cotangent: bfloat16 [4096, 768], P(('dp', 'tensor')), may hold values from -6 to 6
- selected: int32 [4096], P(('dp', 'tensor')), may hold values from 0 to 1, as said below
- buckets: int32 [1023], replicated, may hold values from 0 to 511, as said below
- projector: bfloat16 [3, 768, 768], P(None, 'dp', 'tensor'), may hold values from -0.21875 to 0.21875
- intercepts: bfloat16 [3, 768], P(None, 'tensor')
- combiner: bfloat16 [768, 768], P('dp', 'tensor'), may hold values from -2 to 2
- offset: bfloat16 [768], replicated, may hold values from -1.1953125 to 1.1953125
- relative: bfloat16 [512, 768], replicated, may hold values from -6 to 6
- stretch: float32 [768], replicated, may hold values from 0.5 to 1.5
- uplift: float32 [768], replicated, may hold values from -1.2 to 1.2
- expander: bfloat16 [768, 3072], P(None, 'tensor'), may hold values from -0.21875 to 0.21875
- threshold: bfloat16 [3072], P('tensor'), may hold values from -3 to 3
- reducer: bfloat16 [3072, 768], P('tensor'), may hold values from -0.109375 to 0.109375
- residue: bfloat16 [768], replicated, may hold values from -1.1953125 to 1.1953125
- amplify: float32 [768], replicated, may hold values from 0.5 to 1.5
- displace: float32 [768], replicated, may hold values from -1.2 to 1.2
Outputs:
- result: bfloat16 [4096, 768], P(('dp', 'tensor'))
- tokens_grad: float32 [4096, 768], P(('dp', 'tensor'))
- projector_grad: float32 [3, 768, 768], P(None, 'dp', 'tensor')
- intercepts_grad: float32 [3, 768], P(None, 'tensor')
- combiner_grad: float32 [768, 768], P('dp', 'tensor')
- offset_grad: float32 [768], replicated
- relative_grad: float32 [512, 768], replicated
- stretch_grad: float32 [768], replicated
- uplift_grad: float32 [768], replicated
- expander_grad: float32 [768, 3072], P(None, 'tensor')
- threshold_grad: float32 [3072], P('tensor')
- reducer_grad: float32 [3072, 768], P('tensor')
- residue_grad: float32 [768], replicated
- amplify_grad: float32 [768], replicated
- displace_grad: float32 [768], replicated
Inputs may be any that keep to these rules, and one draw needn't show every extreme that they name: buckets[d + 511] is the bucket of relative offset d. Each aligned quarter of a sequence (128 tokens) has the same number of selected tokens as the other quarters of its sequence, at least 1 and at most 51; in every draw all sequences of some aligned run of 1 sequence have that most in each quarter.
All inputs are finite; a program needn't handle non-finite values.
Results may differ from a plain program's by a relative error of at most 0.019.
Values may be sent and summed in bfloat16 or wider, within the bound.
A program may use at most 128 MiB of HBM per device.

v0:
```python
import math

import jax
import jax.numpy as jnp
from jax import lax
from jax.sharding import PartitionSpec as P

SEQ_LEN = 512
HEAD_DIM = 64


FULL_ACCURACY = lax.Precision.HIGHEST
EPSILON = 1e-05


def normalize(value, gain, shift):
    mean = jnp.mean(value, -1, keepdims=True)
    center = value - mean
    inverse = lax.rsqrt(jnp.mean(center * center, -1, keepdims=True) + EPSILON)
    unit = center * inverse
    return (unit * gain + shift, unit, inverse)


def normalize_back(incoming, gain, unit, inverse):
    scaled = incoming * gain
    result = inverse * (
        scaled
        - jnp.mean(scaled, -1, keepdims=True)
        - unit * jnp.mean(scaled * unit, -1, keepdims=True)
    )
    return (result, jnp.sum(incoming * unit, 0), jnp.sum(incoming, 0))


def gelu_pair(inner):
    cumulative = 0.5 * (1.0 + lax.erf(inner * (1.0 / math.sqrt(2.0))))
    slope = cumulative + inner * jnp.exp(-0.5 * inner * inner) * (1.0 / math.sqrt(2.0 * math.pi))
    return (inner * cumulative, slope)


def skew(spread):
    heads, length, width = spread.shape
    flat = spread[:, :, ::-1].reshape(heads, length * width)
    flat = flat[:, length - 1 : length - 1 + length * (width - 1)]
    return flat.reshape(heads, length, width - 1)[:, :, :length]


def unskew(square):
    heads, length, unused = square.shape
    width = 2 * length - 1
    padded = jnp.pad(square, ((0, 0), (0, 0), (0, length - 2))).reshape(heads, length * (width - 1))
    placed = jnp.pad(padded, ((0, 0), (length - 1, 1)))
    return placed.reshape(heads, length, width)[:, :, ::-1]


def assemble(nearby_unscaled, far_raw, buckets):
    near = skew(jnp.take(nearby_unscaled, buckets, axis=2))
    far = skew(jnp.take(far_raw, buckets, axis=2))
    return near + jnp.swapaxes(far, 1, 2)


def scores_of(query_head_split, key_heads, relative_position_key, pos_query, buckets, scale_factor):
    direct = jnp.einsum(
        "hid,hjd->hij", query_head_split, key_heads, preferred_element_type=jnp.float32
    )
    nearby_unscaled = jnp.einsum(
        "kjo,kao->kja", query_head_split, relative_position_key, preferred_element_type=jnp.float32
    )
    far_raw = jnp.einsum("hjd,hbd->hjb", key_heads, pos_query, preferred_element_type=jnp.float32)
    return (direct + assemble(nearby_unscaled, far_raw, buckets)) * scale_factor


def forward_one(
    query_head_split,
    key_heads,
    value_heads,
    relative_position_key,
    pos_query,
    buckets,
    scale_factor,
):
    scores = scores_of(
        query_head_split, key_heads, relative_position_key, pos_query, buckets, scale_factor
    )
    top = jnp.max(scores, -1, keepdims=True)
    weights = jnp.exp(scores - top)
    total = jnp.sum(weights, -1, keepdims=True)
    probs = weights / total
    context = jnp.einsum(
        "hij,hjd->hid", probs.astype(jnp.bfloat16), value_heads, preferred_element_type=jnp.float32
    )
    return (context.astype(jnp.bfloat16), probs, top + jnp.log(total))


def backward_one(
    query_head_split,
    key_heads,
    value_heads,
    relative_position_key,
    pos_query,
    d_context,
    probs,
    buckets,
    scale_factor,
):
    d_probs = jnp.einsum("hid,hjd->hij", d_context, value_heads, preferred_element_type=jnp.float32)
    d_value = jnp.einsum(
        "hij,hid->hjd", probs.astype(jnp.bfloat16), d_context, preferred_element_type=jnp.float32
    )
    d_scores = (probs * (d_probs - jnp.sum(probs * d_probs, -1, keepdims=True))).astype(
        jnp.bfloat16
    )
    classes = jnp.arange(relative_position_key.shape[1], dtype=jnp.int32)
    indicator_matrix = (buckets[:, None] == classes[None, :]).astype(jnp.bfloat16)
    nearby_spread = unskew(d_scores)
    far_spread = unskew(jnp.swapaxes(d_scores, 1, 2))
    nearby_gradient = (
        jnp.einsum(
            "ctp,pj->ctj", nearby_spread, indicator_matrix, preferred_element_type=jnp.float32
        )
        * scale_factor
    ).astype(jnp.bfloat16)
    d_far = (
        jnp.einsum("hjm,mb->hjb", far_spread, indicator_matrix, preferred_element_type=jnp.float32)
        * scale_factor
    ).astype(jnp.bfloat16)
    d_query = (
        jnp.einsum("hij,hjd->hid", d_scores, key_heads, preferred_element_type=jnp.float32)
        * scale_factor
    )
    d_query = d_query + jnp.einsum(
        "pqr,pry->pqy", nearby_gradient, relative_position_key, preferred_element_type=jnp.float32
    )
    d_key = (
        jnp.einsum("hij,hid->hjd", d_scores, query_head_split, preferred_element_type=jnp.float32)
        * scale_factor
    )
    d_key = d_key + jnp.einsum("hjb,hbd->hjd", d_far, pos_query, preferred_element_type=jnp.float32)
    position_key_gradient = jnp.einsum(
        "ung,uns->ugs", nearby_gradient, query_head_split, preferred_element_type=jnp.float32
    )
    d_pos_query = jnp.einsum("hjb,hjd->hbd", d_far, key_heads, preferred_element_type=jnp.float32)
    return (
        d_query.astype(jnp.bfloat16),
        d_key.astype(jnp.bfloat16),
        d_value.astype(jnp.bfloat16),
        position_key_gradient,
        d_pos_query,
    )


def shards(
    tokens,
    cotangent,
    selected,
    buckets,
    projector,
    intercepts,
    combiner,
    offset,
    relative,
    stretch,
    uplift,
    expander,
    threshold,
    reducer,
    residue,
    amplify,
    displace,
):
    gathered = lax.all_gather(tokens, "tensor", axis=0, tiled=True)
    proj_full, comb_full = (
        lax.all_gather(projector, "dp", axis=1, tiled=True),
        lax.all_gather(combiner, "dp", axis=0, tiled=True),
    )
    head_cols = proj_full.shape[2]
    heads_here = head_cols // HEAD_DIM
    length = SEQ_LEN
    count = gathered.shape[0] // length
    scale_factor = 1.0 / math.sqrt(3 * HEAD_DIM)
    mixed = jnp.einsum("ti,mic->mtc", gathered, proj_full, preferred_element_type=jnp.float32)
    mixed = (mixed + intercepts.astype(jnp.float32)[:, None, :]).astype(jnp.bfloat16)
    positions = jnp.einsum(
        "pi,mic->mpc", relative, proj_full[:2], preferred_element_type=jnp.float32
    )
    positions = (positions + intercepts[:2].astype(jnp.float32)[:, None, :]).astype(jnp.bfloat16)
    pos_query = positions[0].reshape(-1, heads_here, HEAD_DIM).transpose(1, 0, 2)
    relative_position_key = positions[1].reshape(-1, heads_here, HEAD_DIM).transpose(1, 0, 2)
    split_heads = mixed.reshape(3, count, length, heads_here, HEAD_DIM).transpose(0, 1, 3, 2, 4)

    def run_forward(item):
        return forward_one(
            item[0], item[1], item[2], relative_position_key, pos_query, buckets, scale_factor
        )

    def run_light(item):
        outcome = run_forward(item)
        return (outcome[0], outcome[2])

    context_heads, log_totals = lax.map(run_light, (split_heads[0], split_heads[1], split_heads[2]))
    context = context_heads.transpose(0, 2, 1, 3).reshape(count * length, head_cols)
    partial_value = jnp.einsum("tc,oc->to", context, comb_full, preferred_element_type=jnp.float32)
    attended = lax.psum_scatter(
        partial_value.astype(jnp.bfloat16), "tensor", scatter_dimension=0, tiled=True
    ).astype(jnp.float32) + offset.astype(jnp.float32)
    mid, mid_unit, mid_inverse = normalize(tokens.astype(jnp.float32) + attended, stretch, uplift)
    mid_low = mid.astype(jnp.bfloat16)
    hidden_in = lax.all_gather(mid_low, "tensor", axis=0, tiled=True)
    inner = jnp.dot(hidden_in, expander, preferred_element_type=jnp.float32) + threshold.astype(
        jnp.float32
    )
    active, slope = gelu_pair(inner)
    active_low = active.astype(jnp.bfloat16)
    feed_part = jnp.dot(active_low, reducer, preferred_element_type=jnp.float32)
    outer = lax.psum_scatter(
        feed_part.astype(jnp.bfloat16), "tensor", scatter_dimension=0, tiled=True
    ).astype(jnp.float32) + residue.astype(jnp.float32)
    final, end_unit, end_inverse = normalize(mid + outer, amplify, displace)
    result = final.astype(jnp.bfloat16)
    upstream = cotangent.astype(jnp.float32) * selected.astype(jnp.float32)[:, None]
    d_end, amplify_part, displace_part = normalize_back(upstream, amplify, end_unit, end_inverse)
    d_outer = d_end.astype(jnp.bfloat16)
    residue_part = jnp.sum(d_outer.astype(jnp.float32), 0)
    contract_rows = (((0,), (0,)), ((), ()))
    contract_cols = (((1,), (1,)), ((), ()))
    d_rows = lax.all_gather(d_outer, "tensor", axis=0, tiled=True)
    reducer_part = lax.dot_general(
        active_low, d_rows, contract_rows, preferred_element_type=jnp.float32
    )
    d_active = lax.dot_general(d_rows, reducer, contract_cols, preferred_element_type=jnp.float32)
    d_inner = (d_active * slope).astype(jnp.bfloat16)
    expander_part = lax.dot_general(
        hidden_in, d_inner, contract_rows, preferred_element_type=jnp.float32
    )
    threshold_part = jnp.sum(d_inner.astype(jnp.float32), 0)
    back_part = lax.dot_general(
        d_inner, expander, contract_cols, preferred_element_type=jnp.float32
    )
    d_feed = lax.psum_scatter(
        back_part.astype(jnp.bfloat16), "tensor", scatter_dimension=0, tiled=True
    ).astype(jnp.float32)
    d_mid, stretch_part, uplift_part = normalize_back(
        d_end + d_feed, stretch, mid_unit, mid_inverse
    )
    d_attended = d_mid.astype(jnp.bfloat16)
    offset_part = jnp.sum(d_attended.astype(jnp.float32), 0)
    d_attn_rows = lax.all_gather(d_attended, "tensor", axis=0, tiled=True)
    combiner_part = jnp.einsum(
        "to,tc->oc", d_attn_rows, context, preferred_element_type=jnp.float32
    )
    d_context = jnp.dot(d_attn_rows, comb_full, preferred_element_type=jnp.float32).astype(
        jnp.bfloat16
    )
    d_context_heads = d_context.reshape(count, length, heads_here, HEAD_DIM).transpose(0, 2, 1, 3)

    def run_back(item):
        probs = jnp.exp(
            scores_of(item[0], item[1], relative_position_key, pos_query, buckets, scale_factor)
            - item[4]
        )
        return backward_one(
            item[0],
            item[1],
            item[2],
            relative_position_key,
            pos_query,
            item[3],
            probs,
            buckets,
            scale_factor,
        )

    grads = lax.map(
        run_back, (split_heads[0], split_heads[1], split_heads[2], d_context_heads, log_totals)
    )
    d_query_h, d_key_h, d_value_h, d_pos_key_h, d_pos_query_h = grads
    d_mixed = (
        jnp.stack([d_query_h, d_key_h, d_value_h])
        .transpose(0, 1, 3, 2, 4)
        .reshape(3, count * length, head_cols)
    )
    d_pos_query = jnp.sum(d_pos_query_h, 0).transpose(1, 0, 2).reshape(-1, head_cols)
    position_key_gradient = jnp.sum(d_pos_key_h, 0).transpose(1, 0, 2).reshape(-1, head_cols)
    d_positions = jnp.stack([d_pos_query, position_key_gradient])
    projector_part = jnp.einsum(
        "ti,mtc->mic", gathered, d_mixed, preferred_element_type=jnp.float32
    )
    relative_wide = relative.astype(jnp.float32)
    pos_weight = jnp.einsum("pi,mpc->mic", relative_wide, d_positions, precision=FULL_ACCURACY)
    projector_part = projector_part + jnp.concatenate(
        [pos_weight, jnp.zeros((1,) + pos_weight.shape[1:], jnp.float32)], 0
    )
    pos_sums = jnp.sum(d_positions, 1)
    intercept_part = jnp.sum(d_mixed.astype(jnp.float32), 1) + jnp.concatenate(
        [pos_sums, jnp.zeros((1, head_cols), jnp.float32)], 0
    )
    relative_part = jnp.einsum(
        "mpc,mic->pi", d_positions, proj_full[:2].astype(jnp.float32), precision=FULL_ACCURACY
    )
    input_part = jnp.einsum("mtc,mic->ti", d_mixed, proj_full, preferred_element_type=jnp.float32)
    tokens_grad = d_mid + lax.psum_scatter(
        input_part.astype(jnp.bfloat16), "tensor", scatter_dimension=0, tiled=True
    ).astype(jnp.float32)
    projector_grad, combiner_grad = (
        lax.psum_scatter(projector_part, "dp", scatter_dimension=1, tiled=True),
        lax.psum_scatter(combiner_part, "dp", scatter_dimension=0, tiled=True),
    )
    expander_grad, threshold_grad, reducer_grad, intercepts_grad = lax.psum(
        (expander_part, threshold_part, reducer_part, intercept_part), "dp"
    )
    (
        stretch_grad,
        uplift_grad,
        amplify_grad,
        displace_grad,
        offset_grad,
        residue_grad,
        relative_grad,
    ) = lax.psum(
        (
            stretch_part,
            uplift_part,
            amplify_part,
            displace_part,
            offset_part,
            residue_part,
            relative_part,
        ),
        ("dp", "tensor"),
    )
    return (
        result,
        tokens_grad,
        projector_grad,
        intercepts_grad,
        combiner_grad,
        offset_grad,
        relative_grad,
        stretch_grad,
        uplift_grad,
        expander_grad,
        threshold_grad,
        reducer_grad,
        residue_grad,
        amplify_grad,
        displace_grad,
    )


def solution(mesh):
    return jax.shard_map(
        shards,
        mesh=mesh,
        in_specs=(
            P(("dp", "tensor"), None),
            P(("dp", "tensor"), None),
            P(("dp", "tensor")),
            P(),
            P(None, "dp", "tensor"),
            P(None, "tensor"),
            P("dp", "tensor"),
            P(),
            P(),
            P(),
            P(),
            P(None, "tensor"),
            P("tensor"),
            P("tensor", None),
            P(),
            P(),
            P(),
        ),
        out_specs=(
            P(("dp", "tensor"), None),
            P(("dp", "tensor"), None),
            P(None, "dp", "tensor"),
            P(None, "tensor"),
            P("dp", "tensor"),
            P(),
            P(),
            P(),
            P(),
            P(None, "tensor"),
            P("tensor"),
            P("tensor", None),
            P(),
            P(),
            P(),
        ),
        check_vma=False,
    )
```

profile of v0, /device:TPU:0, one launch (start us, length us, event | category | flops | bytes accessed | tf_op | source)
XLA Modules:
  0.0 1036.4 jit_solution(10009907324415564357)
XLA Ops:
  11.2 38.7 %all_gather.18 = bf16[3,768,192]{2,0,1:T(4,128)(2,1)S(1)} all-gather(bf16[3,96,192]{2,0,1:T(4,128)(2,1)S(1)} %copy.84), channel_id=1, replica_groups=mesh['dp'=8,'tensor'=4] {'dp'}, dimensions={1}, use_global_device_ids=true | all-gather | bytes 995328 | tf_op jit(solution)/shard_map/all_gather | solution.py:172
  51.9 8.7 all_gather.19
  78.3 15.5 %gather_fusion = f32[1023,3,512]{2,1,0:T(4,128)} fusion(f32[3,512,512]{1,0,2:T(4,128)} %copy.88, s32[1024]{0:T(1024)S(1)} %pad_clamp_fusion), kind=kCustom, calls=%fused_computation.clone | custom fusion | bytes 12574716 | tf_op jit(solution)/shard_map/while/body/eval_jaxpr/jit(_take)/gather | solution.py:56
  93.9 15.6 %gather_fusion.1 = f32[1023,3,512]{2,1,0:T(4,128)} fusion(f32[3,512,512]{1,0,2:T(4,128)} %copy.91, s32[1024]{0:T(1024)S(1)} %pad_clamp_fusion), kind=kCustom, calls=%fused_computation.1.clone | custom fusion | bytes 12574716 | tf_op jit(solution)/shard_map/while/body/eval_jaxpr/jit(_take)/gather | solution.py:57
  109.5 13.7 %select_bitcast_fusion = (f32[3,512,1023]{1,0,2:T(4,128)}, f32[3,512,1023]{1,0,2:T(4,128)}) fusion(f32[1023,3,512]{2,1,0:T(4,128)} %gather_fusion.1, pred[1023]{0:T(1024)(128)(4,1)S(1)} %compare_and_fusion, f32[1023,3,512]{2,1,0:T(4,128)} %gather_fusion), kind=kLoop, calls=%fused_computation.2 | loop fusion | flops 3142656 | bytes 25142272 | tf_op jit(solution)/shard_map/while/body/eval_jaxpr/jit(_take)/select_n | solution.py:57
  123.1 8.1 rev.20
  131.2 9.3 copy.89
  140.5 13.4 %reshape.163 = f32[3,523776]{1,0:T(4,128)} reshape(f32[3,512,1023]{2,1,0:T(8,128)} %copy.89) | data formatting | bytes 12570624 | tf_op jit(solution)/shard_map/while/body/eval_jaxpr/reshape | solution.py:42
  153.9 9.5 slice.68
  163.4 13.4 %reshape.164 = f32[3,512,1022]{2,1,0:T(8,128)} reshape(f32[3,523264]{1,0:T(4,128)} %slice.68) | data formatting | bytes 12558336 | tf_op jit(solution)/shard_map/while/body/eval_jaxpr/reshape | solution.py:44
  184.2 8.1 rev.21
  192.3 9.6 copy.92
  201.8 13.4 %reshape.165 = f32[3,523776]{1,0:T(4,128)} reshape(f32[3,512,1023]{2,1,0:T(8,128)} %copy.92) | data formatting | bytes 12570624 | tf_op jit(solution)/shard_map/while/body/eval_jaxpr/reshape | solution.py:42
  215.2 9.4 slice.71
  224.6 13.4 %reshape.166 = f32[3,512,1022]{2,1,0:T(8,128)} reshape(f32[3,523264]{1,0:T(4,128)} %slice.71) | data formatting | bytes 12558336 | tf_op jit(solution)/shard_map/while/body/eval_jaxpr/reshape | solution.py:44
  243.2 31.2 %all_gather.20 = bf16[768,192]{1,0:T(8,128)(2,1)S(1)} all-gather(bf16[96,192]{1,0:T(8,128)(2,1)S(1)} %copy-done.45), channel_id=1, replica_groups=mesh['dp'=8,'tensor'=4] {'dp'}, dimensions={0}, use_global_device_ids=true | all-gather | bytes 331776 | tf_op jit(solution)/shard_map/all_gather | solution.py:173
  275.8 21.4 %reduce-scatter.9.cloned.1.call-done = bf16[128,768]{1,0:T(8,128)(2,1)} async-done(((bf16[512,768]{1,0:T(8,128)(2,1)}), bf16[128,768]{1,0:T(8,128)(2,1)}) %reduce-scatter.9.cloned.1.call-update) | async-done | bytes 196624 | tf_op jit(solution)/shard_map/reduce_scatter | solution.py:202
  300.5 8.0 all_gather.21
  312.4 23.8 %reduce-scatter.11.cloned.1.call-done = bf16[128,768]{1,0:T(8,128)(2,1)} async-done(((bf16[512,768]{1,0:T(8,128)(2,1)}), bf16[128,768]{1,0:T(8,128)(2,1)}) %reduce-scatter.11.cloned.1.call-update) | async-done | bytes 196624 | tf_op jit(solution)/shard_map/reduce_scatter | solution.py:214
  340.3 8.2 all_gather.22
  352.0 23.9 %reduce-scatter.13.cloned.1.call-done = bf16[128,768]{1,0:T(8,128)(2,1)} async-done(((bf16[512,768]{1,0:T(8,128)(2,1)}), bf16[128,768]{1,0:T(8,128)(2,1)}) %reduce-scatter.13.cloned.1.call-update) | async-done | bytes 196624 | tf_op jit(solution)/shard_map/reduce_scatter | solution.py:238
  380.6 8.0 all_gather.23
  402.8 7.8 reshape.207
  428.8 6.8 reshape.170
  435.7 34.0 %reverse.1 = bf16[3,512,1024]{2,1,0:T(8,128)(2,1)} reverse(bf16[3,512,1024]{2,1,0:T(8,128)(2,1)S(1)} %bitcast.143), dimensions={2} | reverse | bytes 6291456
  475.6 7.8 reshape.203
  508.3 33.9 %reverse = bf16[3,512,1024]{2,1,0:T(8,128)(2,1)} reverse(bf16[3,512,1024]{2,1,0:T(8,128)(2,1)S(1)} %bitcast.144), dimensions={2} | reverse | bytes 6291456
  574.8 41.3 %all-reduce.6 = (f32[768]{0:T(1024)}, f32[768]{0:T(1024)}, f32[768]{0:T(1024)}, f32[768]{0:T(1024)}, f32[768]{0:T(1024)}, /*index=5*/f32[768]{0:T(1024)}) all-reduce(f32[768]{0:T(1024)S(1)} %copy-done.53, f32[768]{0:T(1024)S(1)} %copy-done.51, f32[768]{0:T(1024)S(1)} %copy-done.52, ...), channel_id=1, replica_groups=mesh['dp'=8,'tensor'=4] {'dp','tensor'}, use_global_device_ids=true, to_apply=%region_21.23 | all-reduce | flops 4608 | bytes 36864 | tf_op jit(solution)/shard_map/psum | solution.py:318
  616.2 22.4 %all-reduce.7 = (f32[3,192]{1,0:T(4,128)}, f32[768]{0:T(1024)}) all-reduce(f32[3,192]{1,0:T(4,128)S(1)} %pad_add_fusion, f32[768]{0:T(1024)S(1)} %copy-done.58), channel_id=1, replica_groups=mesh['dp'=8,'tensor'=4] {'dp'}, use_global_device_ids=true, to_apply=%region_18.20 | all-reduce | flops 1344 | bytes 10752 | tf_op jit(solution)/shard_map/psum | solution.py:307
  648.1 135.5 %all-reduce.12.cloned.1.call-done = f32[512,768]{1,0:T(8,128)} async-done(((f32[512,768]{1,0:T(8,128)}), f32[512,768]{1,0:T(8,128)}) %all-reduce.12.cloned.1.call-update) | async-done | bytes 1572880 | tf_op jit(solution)/shard_map/psum | solution.py:318
  783.6 66.1 %reduce-scatter.17.cloned.1.call-done = f32[96,192]{1,0:T(8,128)} async-done(((f32[768,192]{1,0:T(8,128)}), f32[96,192]{1,0:T(8,128)}) %reduce-scatter.17.cloned.1.call-update) | async-done | bytes 73744 | tf_op jit(solution)/shard_map/reduce_scatter | solution.py:305
  849.7 172.7 %all-reduce.14.cloned.1.call-done = (f32[768,768]{1,0:T(8,128)}, f32[768,768]{1,0:T(8,128)}) async-done(((f32[768,768]{1,0:T(8,128)}, f32[768,768]{1,0:T(8,128)}), (f32[768,768]{1,0:T(8,128)}, f32[768,768]{1,0:T(8,128)})) %all-reduce.14.cloned.1.call-update) | async-done | bytes 4718608 | tf_op jit(solution)/shard_map/psum | solution.py:307
  (236 shorter events, 168.5 us)
Async XLA Ops:
  7.2 301.4 %copy-start = (bf16[768,768]{1,0:T(8,128)(2,1)S(1)}, bf16[768,768]{1,0:T(8,128)(2,1)}, u32[]{:S(2)}) copy-start(bf16[768,768]{1,0:T(8,128)(2,1)} %param.30) | copy-start | bytes 3538948
  7.2 44.7 %copy-start.6 = (bf16[128,768]{1,0:T(8,128)(2,1)S(1)}, bf16[128,768]{1,0:T(8,128)(2,1)}, u32[]{:S(2)}) copy-start(bf16[128,768]{1,0:T(8,128)(2,1)} %param.19) | copy-start | bytes 589828
  7.2 290.0 %reduce-scatter.9.cloned.1.call-start = ((), (), s32[]{:S(2)}) async-start(), calls=%async_computation.6 | async-start | bytes 983040 | tf_op jit(solution)/shard_map/reduce_scatter | solution.py:202
  63.5 178.5 %copy-start.16 = (bf16[3,192,512]{2,1,0:T(8,128)(2,1)}, bf16[3,192,512]{2,1,0:T(8,128)(2,1)S(1)}, u32[]{:S(2)}) copy-start(bf16[3,192,512]{2,1,0:T(8,128)(2,1)S(1)} %fusion.24) | copy-start | bytes 1769476
  243.1 56.3 %copy-start.40 = (bf16[3,512,64]{1,2,0:T(8,128)(2,1)}, bf16[3,512,64]{1,2,0:T(8,128)(2,1)S(1)}, u32[]{:S(2)}) copy-start(bf16[3,512,64]{1,2,0:T(8,128)(2,1)S(1)} %fusion.29) | copy-start | bytes 589828
  243.1 32.6 %copy-start.59 = (bf16[768]{0:T(1024)(128)(2,1)S(1)}, bf16[768]{0:T(1024)(128)(2,1)}, u32[]{:S(2)}) copy-start(bf16[768]{0:T(1024)(128)(2,1)} %param.26) | copy-start | bytes 4612
  243.1 32.7 %copy-start.60 = (bf16[768]{0:T(1024)(128)(2,1)S(1)}, bf16[768]{0:T(1024)(128)(2,1)}, u32[]{:S(2)}) copy-start(bf16[768]{0:T(1024)(128)(2,1)} %param.31) | copy-start | bytes 4612
  243.1 56.3 %copy-start.44 = (f32[768]{0:T(1024)S(1)}, f32[768]{0:T(1024)}, u32[]{:S(2)}) copy-start(f32[768]{0:T(1024)} %param.28) | copy-start | bytes 9220
  243.2 56.3 %copy-start.46 = (f32[768]{0:T(1024)S(1)}, f32[768]{0:T(1024)}, u32[]{:S(2)}) copy-start(f32[768]{0:T(1024)} %param.29) | copy-start | bytes 9220
  274.4 25.0 %copy-start.17 = (bf16[768,192]{1,0:T(8,128)(2,1)}, bf16[768,192]{1,0:T(8,128)(2,1)S(1)}, u32[]{:S(2)}) copy-start(bf16[768,192]{1,0:T(8,128)(2,1)S(1)} %all_gather.20) | copy-start | bytes 884740
  275.7 60.5 %reduce-scatter.11.cloned.1.call-start = ((), (), s32[]{:S(2)}) async-start(), calls=%async_computation.7 | async-start | bytes 983040 | tf_op jit(solution)/shard_map/reduce_scatter | solution.py:214
  298.3 38.0 %copy-start.55 = (f32[128]{0:T(128)}, f32[128]{0:T(128)S(1)}, u32[]{:S(2)}) copy-start(f32[128]{0:T(128)S(1)} %broadcast_multiply_fusion.5) | copy-start | bytes 1540
  299.5 36.8 %copy-start.56 = (f32[128]{0:T(128)}, f32[128]{0:T(128)S(1)}, u32[]{:S(2)}) copy-start(f32[128]{0:T(128)S(1)} %add_rsqrt_fusion.1) | copy-start | bytes 1540
  310.6 27.0 %copy-start.29 = (bf16[512,768]{1,0:T(8,128)(2,1)}, bf16[512,768]{1,0:T(8,128)(2,1)S(1)}, u32[]{:S(2)}) copy-start(bf16[512,768]{1,0:T(8,128)(2,1)S(1)} %get-tuple-element.180) | copy-start | bytes 2359300
  310.6 25.7 %copy-start.9 = (bf16[128,768]{1,0:T(8,128)(2,1)S(1)}, bf16[128,768]{1,0:T(8,128)(2,1)}, u32[]{:S(2)}) copy-start(bf16[128,768]{1,0:T(8,128)(2,1)} %reduce-scatter.9.cloned.1.call-done) | copy-start | bytes 589828
  310.6 27.2 %copy-start.38 = (bf16[128,768]{1,0:T(8,128)(2,1)S(1)}, bf16[128,768]{1,0:T(8,128)(2,1)}, u32[]{:S(2)}) copy-start(bf16[128,768]{1,0:T(8,128)(2,1)} %param.20) | copy-start | bytes 589828
  310.6 27.2 %copy-start.47 = (f32[768]{0:T(1024)S(1)}, f32[768]{0:T(1024)}, u32[]{:S(2)}) copy-start(f32[768]{0:T(1024)} %param.34) | copy-start | bytes 9220
  310.7 28.0 %copy-start.57 = (f32[768]{0:T(1024)S(1)}, f32[768]{0:T(1024)}, u32[]{:S(2)}) copy-start(f32[768]{0:T(1024)} %param.35) | copy-start | bytes 9220
  312.3 63.5 %reduce-scatter.13.cloned.1.call-start = ((), (), s32[]{:S(2)}) async-start(), calls=%async_computation.8 | async-start | bytes 983040 | tf_op jit(solution)/shard_map/reduce_scatter | solution.py:238
  336.3 12.2 %copy-start.63 = (bf16[768,768]{1,0:T(8,128)(2,1)S(1)}, bf16[768,768]{1,0:T(8,128)(2,1)}, u32[]{:S(2)}) copy-start(bf16[768,768]{1,0:T(8,128)(2,1)} %param.32) | copy-start | bytes 3538948
  336.3 12.2 %copy-start.65 = (f32[512,768]{1,0:T(8,128)S(1)}, f32[512,768]{1,0:T(8,128)}, u32[]{:S(2)}) copy-start(f32[512,768]{1,0:T(8,128)} %get-tuple-element.181) | copy-start | bytes 4718596
  350.2 25.6 %copy-start.42 = (bf16[512,768]{1,0:T(8,128)(2,1)}, bf16[512,768]{1,0:T(8,128)(2,1)S(1)}, u32[]{:S(2)}) copy-start(bf16[512,768]{1,0:T(8,128)(2,1)S(1)} %get-tuple-element.185) | copy-start | bytes 2359300
  351.9 286.6 %reduce-scatter.15.cloned.1.call-start = ((), (), s32[]{:S(2)}) async-start(), calls=%async_computation.9 | async-start | bytes 983040 | tf_op jit(solution)/shard_map/reduce_scatter | solution.py:300
  375.9 14.4 %copy-start.3 = (f32[3,512,512]{1,2,0:T(8,128)S(1)}, f32[3,512,512]{1,2,0:T(8,128)}, u32[]{:S(2)}) copy-start(f32[3,512,512]{1,2,0:T(8,128)} %copy-done.2) | copy-start | bytes 9437188
  435.7 34.1 %copy-start.54 = (s32[1023]{0:T(1024)S(1)}, s32[1023]{0:T(1024)}, u32[]{:S(2)}) copy-start(s32[1023]{0:T(1024)} %param.22) | copy-start | bytes 12280
  550.8 95.4 %reduce-scatter.19.cloned.1.call-start = ((), (), s32[]{:S(2)}) async-start(), calls=%async_computation.12 | async-start | bytes 2211840
  563.3 220.4 %all-reduce.12.cloned.1.call-start = ((), (), s32[]{:S(2)}) async-start(), calls=%async_computation.11 | async-start | bytes 3145728 | tf_op jit(solution)/shard_map/psum | solution.py:318
  568.1 281.7 %reduce-scatter.17.cloned.1.call-start = ((), (), s32[]{:S(2)}) async-start(), calls=%async_computation.10 | async-start | bytes 884736 | tf_op jit(solution)/shard_map/reduce_scatter | solution.py:305
  569.5 453.0 %all-reduce.14.cloned.1.call-start = ((), (), s32[]{:S(2)}) async-start(), calls=%async_computation.13 | async-start | bytes 9437184 | tf_op jit(solution)/shard_map/psum | solution.py:307
  574.0 42.0 %copy-start.13 = (f32[3,512,64]{1,2,0:T(8,128)S(1)}, f32[3,512,64]{1,2,0:T(8,128)}, u32[]{:S(2)}) copy-start(f32[3,512,64]{1,2,0:T(8,128)} %copy-done.12) | copy-start | bytes 1179652
  574.0 42.2 %copy-start.58 = (f32[768]{0:T(1024)S(1)}, f32[768]{0:T(1024)}, u32[]{:S(2)}) copy-start(f32[768]{0:T(1024)} %get-tuple-element.184) | copy-start | bytes 9220
  574.0 64.6 %copy-start.35 = (f32[128,768]{1,0:T(8,128)S(1)}, f32[128,768]{1,0:T(8,128)}, u32[]{:S(2)}) copy-start(f32[128,768]{1,0:T(8,128)} %get-tuple-element.168) | copy-start | bytes 1179652
  (42 other events, 109.3 us)
Sparse Core Ops, SparseCore 0:
  275.9 21.3 reduce-scatter.8
  312.5 23.7 reduce-scatter.10
  352.1 23.7 reduce-scatter.12
  550.9 23.7 reduce-scatter.14
  578.0 68.1 reduce-scatter.18
  651.9 131.6 all-reduce.11
  787.5 62.1 reduce-scatter.16
  853.9 168.4 all-reduce.13
where the time goes:
time: 1040 us
  waiting for transfers between devices  449 us (43%)
  local copies, waits for them, and re-layouts  315 us (30%)
  blocking collectives  167 us (16%)
  matrix products  56.7 us (5%)
  other arithmetic  33 us (3%)
  between operations  15.4 us (1%)
    psum x1, waiting for transfers between devices, shards(): lax.psum((expander_part, threshold_part, reducer_part, intercept_part), '...  173 us
    psum x1, waiting for transfers between devices, shards(): lax.psum((stretch_part, uplift_part, amplify_part, displace_part, offset_...  136 us
    unnamed x148, local copies, waits for them, and re-layouts  122 us
    reduce_scatter x1, waiting for transfers between devices, shards(): lax.psum_scatter(combiner_part, 'dp', scatter_dimension=0, tiled=True)  66.1 us
    psum x1, blocking collectives, shards(): lax.psum((stretch_part, uplift_part, amplify_part, displace_part, offset_...  41.3 us
    all_gather x1, blocking collectives, shards(): lax.all_gather(projector, 'dp', axis=1, tiled=True)  38.7 us
    rev x4, local copies, waits for them, and re-layouts, skew(): flat = spread[:, :, ::-1].reshape(heads, length * width)  35 us
    all_gather x1, blocking collectives, shards(): lax.all_gather(combiner, 'dp', axis=0, tiled=True)  31.2 us
  transfers between devices with their start and end apart: 8, of which 7 were waited for; matrix products, arithmetic and copies ran while one was open for 2% of the time, Pallas kernels for 0%

commit v1 on v0

v1 whole, which is shorter than its diff:
```python
import functools
import math

import jax, jax.numpy as jnp
from jax import lax
from jax.experimental import pallas as pl
from jax.experimental.pallas import tpu as pltpu
from jax.sharding import PartitionSpec as P

HEAD_DIM = 64
BLK = 128
F32, BF16 = jnp.float32, jnp.bfloat16

def nn(a, b):
    return lax.dot_general(a, b, (((1,), (0,)), ((), ())), preferred_element_type=F32)

def nt(a, b):
    return lax.dot_general(a, b, (((1,), (1,)), ((), ())), preferred_element_type=F32)

def tn(a, b):
    return lax.dot_general(a, b, (((0,), (0,)), ((), ())), preferred_element_type=F32)

def attn_fwd_kernel(scale, x_ref, w_ref, bias_ref, rel_ref, bcol_ref,
                    probs_ref, mixed_ref, table_ref, ctx_ref, part_ref, far_ref, acc_ref):
    length = x_ref.shape[0]
    cols = ctx_ref.shape[1]
    classes = rel_ref.shape[0]
    span = table_ref.shape[0]
    blocks = length // BLK
    win = length + BLK
    bias = bias_ref[...].astype(F32)
    mixed_ref[...] = (nn(x_ref[...], w_ref[:, : 3 * cols]) + bias).astype(BF16)
    pos = (nn(rel_ref[...], w_ref[:, : 2 * cols]) + bias[:, : 2 * cols]).astype(BF16)
    spread = (bcol_ref[...] == lax.broadcasted_iota(jnp.int32, (span, classes), 1)).astype(BF16)
    table_ref[...] = nn(spread, pos).astype(BF16)
    lanes = lax.broadcasted_iota(jnp.int32, (1, cols), 1) // HEAD_DIM
    acc_ref[...] = jnp.zeros_like(acc_ref)

    def head(h, carry):
        own = lanes == h
        pick = lambda v: jnp.where(own, v, jnp.zeros_like(v))
        key_h = pick(mixed_ref[:, cols : 2 * cols])
        for b in range(blocks):
            start = length - BLK * (b + 1)
            rows = slice(BLK * b, BLK * (b + 1))
            wide = nt(key_h[rows], table_ref[start : start + win, :cols])
            turned = pltpu.roll(wide, win - BLK + 1, 1, stride=1, stride_axis=0)[:, :length]
            far_ref[:, rows] = turned.T
        value_h = pick(mixed_ref[:, 2 * cols : 3 * cols])
        for b in range(blocks):
            start = length - BLK * (b + 1)
            rows = slice(BLK * b, BLK * (b + 1))
            query = pick(mixed_ref[rows, :cols])
            wide = nt(query, table_ref[start : start + win, cols : 2 * cols])
            near = pltpu.roll(wide, win - BLK + 1, 1, stride=1, stride_axis=0)[:, :length]
            scores = (nt(query, key_h) + near + far_ref[rows, :]) * scale
            top = jnp.max(scores, -1, keepdims=True)
            weights = jnp.exp(scores - top)
            probs = weights / jnp.sum(weights, -1, keepdims=True)
            probs_ref[h, rows, :] = probs
            acc_ref[rows, :] += nn(probs.astype(BF16), value_h)
        return carry

    lax.fori_loop(0, cols // HEAD_DIM, head, 0)
    ctx_ref[...] = acc_ref[...].astype(BF16)
    part_ref[...] = nt(ctx_ref[...], w_ref[:, 3 * cols :]).astype(BF16)

def attn_fwd(x, w, bias, rel, bcol):
    length = x.shape[0]
    cols = w.shape[1] // 4
    width = w.shape[0]
    scale = 1.0 / math.sqrt(3 * HEAD_DIM)
    heads = cols // HEAD_DIM
    span = bcol.shape[0]
    S = jax.ShapeDtypeStruct
    return pl.pallas_call(
        functools.partial(attn_fwd_kernel, scale),
        out_shape=(S((heads, length, length), F32), S((length, 3 * cols), BF16), S((span, 2 * cols), BF16),
                   S((length, cols), BF16), S((length, width), BF16)),
        scratch_shapes=[pltpu.VMEM((length, length), F32), pltpu.VMEM((length, cols), F32)],
        name="attn_fwd",
    )(x, w, bias, rel, bcol)

def attn_bwd_kernel(scale, x_ref, w_ref, rel_ref, bcol_ref, probs_ref, mixed_ref, table_ref, ctx_ref, rows_ref, sel_ref,
                    grads_ref, part_ref, relpart_ref, bias_ref,
                    dctx_ref, dctx_t, turn_t, dq_ref, dk_ref, dv_t, dpos_t, ds_ref):
    length = x_ref.shape[0]
    cols = ctx_ref.shape[1]
    classes = rel_ref.shape[0]
    span = table_ref.shape[0]
    blocks = length // BLK
    win = length + BLK
    keep = sel_ref.shape[0] // blocks
    flip = (lax.broadcasted_iota(jnp.int32, (BLK, BLK), 0) + lax.broadcasted_iota(jnp.int32, (BLK, BLK), 1) == BLK - 1).astype(BF16)
    small = nn(rows_ref[...], w_ref[:, 3 * cols :]).astype(BF16)
    ctx_small = []
    for b in range(blocks):
        rows = slice(BLK * b, BLK * (b + 1))
        few = slice(keep * b, keep * (b + 1))
        dctx_ref[rows, :] = tn(sel_ref[few, :], small[few]).astype(BF16)
        ctx_small.append(nn(sel_ref[few, :], ctx_ref[rows, :]).astype(BF16))
        turn_t[:cols, rows] = tn(mixed_ref[rows, :cols], flip).astype(BF16)
        turn_t[cols:, rows] = tn(mixed_ref[rows, cols : 2 * cols], flip).astype(BF16)
    dctx_t[...] = dctx_ref[...].T
    grads_ref[:, 3 * cols :] = tn(rows_ref[...], jnp.concatenate(ctx_small, 0)).astype(BF16)
    lanes = lax.broadcasted_iota(jnp.int32, (1, cols), 1) // HEAD_DIM
    dq_ref[...] = jnp.zeros_like(dq_ref)
    dk_ref[...] = jnp.zeros_like(dk_ref)
    dpos_t[...] = jnp.zeros_like(dpos_t)
    blank = jnp.zeros((BLK, BLK), F32)

    def head(h, carry):
        own = lanes == h
        pick = lambda v: jnp.where(own, v, jnp.zeros_like(v))
        mine = pl.ds(pl.multiple_of(h * HEAD_DIM, HEAD_DIM), HEAD_DIM)
        key_h = pick(mixed_ref[:, cols : 2 * cols])
        query_h = pick(mixed_ref[:, :cols])
        value = mixed_ref[:, 2 * cols : 3 * cols]
        posq_h = pick(table_ref[:, :cols])
        posk_h = pick(table_ref[:, cols : 2 * cols])
        total = jnp.zeros((HEAD_DIM, length), F32)
        for b in range(blocks):
            start = length - BLK * (b + 1)
            rows = slice(BLK * b, BLK * (b + 1))
            probs = probs_ref[h, rows, :]
            dprobs = nt(pick(dctx_ref[rows, :]), value)
            dscores = (probs * (dprobs - jnp.sum(probs * dprobs, -1, keepdims=True))).astype(BF16)
            ds_ref[rows, :] = dscores
            total += nn(dctx_t[mine, rows], probs.astype(BF16))
            turned = nn(flip, dscores)
            moved = pltpu.roll(jnp.concatenate([turned, blank], 1), 0, 1, stride=1, stride_axis=0).astype(BF16)
            dq_ref[rows, :] += nn(turned.astype(BF16), key_h) + nn(moved, posk_h[start : start + win])
            low = pl.ds(pl.multiple_of(cols + h * HEAD_DIM, HEAD_DIM), HEAD_DIM)
            dpos_t[low, start : start + win] += nn(turn_t[mine, rows], moved)
        dv_t[mine, :] = total
        for b in range(blocks):
            start = length - BLK * (b + 1)
            rows = slice(BLK * b, BLK * (b + 1))
            turned = nt(flip, ds_ref[:, rows])
            moved = pltpu.roll(jnp.concatenate([turned, blank], 1), 0, 1, stride=1, stride_axis=0).astype(BF16)
            dk_ref[rows, :] += nn(turned.astype(BF16), query_h) + nn(moved, posq_h[start : start + win])
            low = pl.ds(pl.multiple_of(cols + h * HEAD_DIM, HEAD_DIM), HEAD_DIM)
            dpos_t[mine, start : start + win] += nn(turn_t[low, rows], moved)
        return carry

    lax.fori_loop(0, cols // HEAD_DIM, head, 0)
    order = lambda ref: jnp.concatenate([nn(flip, (ref[BLK * b : BLK * (b + 1), :] * scale).astype(BF16)).astype(BF16) for b in range(blocks)], 0)
    dmixed = jnp.concatenate([order(dq_ref), order(dk_ref), dv_t[...].T.astype(BF16)], 1)
    spread = (bcol_ref[...] == lax.broadcasted_iota(jnp.int32, (span, classes), 1)).astype(BF16)
    wide = dpos_t[...] * scale
    high = wide.astype(BF16)
    dpos = (nn(high, spread) + nn((wide - high.astype(F32)).astype(BF16), spread)).T
    dpos_low = dpos.astype(BF16)
    sums = jnp.sum(dmixed.astype(F32), 0, keepdims=True)
    bias_ref[...] = sums
    bias_ref[:, : 2 * cols] += jnp.sum(dpos, 0, keepdims=True)
    relpart_ref[...] = nt(dpos_low, w_ref[:, : 2 * cols]).astype(BF16)
    part_ref[...] = nt(dmixed, w_ref[:, : 3 * cols]).astype(BF16)
    both = tn(x_ref[...], dmixed)
    grads_ref[:, : 2 * cols] = (both[:, : 2 * cols] + tn(rel_ref[...], dpos_low)).astype(BF16)
    grads_ref[:, 2 * cols : 3 * cols] = both[:, 2 * cols :].astype(BF16)

def attn_bwd(x, w, rel, bcol, probs, mixed, table, ctx, rows, sel):
    length, width = x.shape
    cols = w.shape[1] // 4
    scale = 1.0 / math.sqrt(3 * HEAD_DIM)
    span = bcol.shape[0]
    S = jax.ShapeDtypeStruct
    V = pltpu.VMEM
    return pl.pallas_call(
        functools.partial(attn_bwd_kernel, scale),
        out_shape=(S((width, 4 * cols), BF16), S((length, width), BF16), S((rel.shape[0], width), BF16), S((1, 3 * cols), F32)),
        scratch_shapes=[V((length, cols), BF16), V((cols, length), BF16), V((2 * cols, length), BF16), V((length, cols), F32), V((length, cols), F32),
                        V((cols, length), F32), V((2 * cols, span), F32), V((length, length), BF16)],
        name="attn_bwd",
    )(x, w, rel, bcol, probs, mixed, table, ctx, rows, sel)


EPSILON = 1e-05


def normalize(value, gain, shift):
    mean = jnp.mean(value, -1, keepdims=True)
    center = value - mean
    inverse = lax.rsqrt(jnp.mean(center * center, -1, keepdims=True) + EPSILON)
    unit = center * inverse
    return (unit * gain + shift, unit, inverse)


def normalize_back(incoming, gain, unit, inverse):
    scaled = incoming * gain
    result = inverse * (
        scaled
        - jnp.mean(scaled, -1, keepdims=True)
        - unit * jnp.mean(scaled * unit, -1, keepdims=True)
    )
    return (result, jnp.sum(incoming * unit, 0), jnp.sum(incoming, 0))


def cumulative(inner):
    return 0.5 * (1.0 + lax.erf(inner * (1.0 / math.sqrt(2.0))))


def shards(tokens, cotangent, selected, buckets, projector, intercepts, combiner, offset, relative, stretch, uplift,
           expander, threshold, reducer, residue, amplify, displace):
    quarter, width = tokens.shape
    cols = projector.shape[2]
    group = lax.axis_size("tensor")
    keep = -(-(quarter * 2 // 5) // 16) * 16
    x = lax.all_gather(tokens, "tensor", axis=0, tiled=True)
    packed = jnp.concatenate([projector[0], projector[1], projector[2], combiner], 1)
    w = lax.all_gather(packed, "dp", axis=0, tiled=True)
    chosen = lax.all_gather(selected, "tensor", axis=0, tiled=True).reshape(group, quarter)
    rank = jnp.cumsum(chosen, 1) - 1
    sel = ((rank[:, None, :] == jnp.arange(keep, dtype=jnp.int32)[None, :, None]) & (chosen[:, None, :] == 1)).astype(BF16)
    mine = lax.dynamic_index_in_dim(sel, lax.axis_index("tensor"), 0, keepdims=False)
    sel_flat = sel.reshape(group * keep, quarter)
    bias = intercepts.reshape(1, 3 * cols)
    span = buckets.shape[0] + 1
    bcol = jnp.concatenate([buckets[::-1], jnp.full((1,), -1, jnp.int32)]).reshape(span, 1)
    probs, mixed, table, ctx, part = attn_fwd(x, w, bias, relative, bcol)
    attended = lax.psum_scatter(part, "tensor", scatter_dimension=0, tiled=True).astype(F32) + offset.astype(F32)
    mid, mid_unit, mid_inverse = normalize(tokens.astype(F32) + attended, stretch, uplift)
    hidden_in = lax.all_gather(mid.astype(BF16), "tensor", axis=0, tiled=True)
    bent = threshold.astype(F32)
    inner = nn(hidden_in, expander) + bent
    active = (inner * cumulative(inner)).astype(BF16)
    feed = nn(active, reducer).astype(BF16)
    outer = lax.psum_scatter(feed, "tensor", scatter_dimension=0, tiled=True).astype(F32) + residue.astype(F32)
    final, end_unit, end_inverse = normalize(mid + outer, amplify, displace)
    upstream = cotangent.astype(F32) * selected.astype(F32)[:, None]
    d_end, amplify_part, displace_part = normalize_back(upstream, amplify, end_unit, end_inverse)
    d_outer = d_end.astype(BF16)
    residue_part = jnp.sum(d_outer.astype(F32), 0)
    d_rows = lax.all_gather(nn(mine, d_outer).astype(BF16), "tensor", axis=0, tiled=True)
    few = lax.dot_general(sel, hidden_in.reshape(group, quarter, width), (((2,), (1,)), ((0,), (0,))), preferred_element_type=F32)
    few = few.astype(BF16).reshape(group * keep, width)
    inner_few = nn(few, expander) + bent
    weight = cumulative(inner_few)
    active_few = (inner_few * weight).astype(BF16)
    slope = weight + inner_few * jnp.exp(-0.5 * inner_few * inner_few) * (1.0 / math.sqrt(2.0 * math.pi))
    d_inner = (nt(d_rows, reducer) * slope).astype(BF16)
    reducer_part = tn(active_few, d_rows).astype(BF16)
    expander_part = tn(few, d_inner).astype(BF16)
    threshold_part = jnp.sum(d_inner.astype(F32), 0)
    back = nt(d_inner, expander).astype(BF16)
    d_feed_few = lax.psum_scatter(back, "tensor", scatter_dimension=0, tiled=True)
    d_feed = tn(mine, d_feed_few)
    d_mid, stretch_part, uplift_part = normalize_back(d_end + d_feed, stretch, mid_unit, mid_inverse)
    d_attended = d_mid.astype(BF16)
    offset_part = jnp.sum(d_attended.astype(F32), 0)
    d_attn = lax.all_gather(nn(mine, d_attended).astype(BF16), "tensor", axis=0, tiled=True)
    grads, input_part, rel_part, bias_part = attn_bwd(x, w, relative, bcol, probs, mixed, table, ctx, d_attn, sel_flat)
    tokens_grad = d_mid + lax.psum_scatter(input_part, "tensor", scatter_dimension=0, tiled=True).astype(F32)
    mine_grads = lax.psum_scatter(grads, "dp", scatter_dimension=0, tiled=True).astype(F32)
    projector_grad = jnp.stack([mine_grads[:, :cols], mine_grads[:, cols : 2 * cols], mine_grads[:, 2 * cols : 3 * cols]])
    combiner_grad = mine_grads[:, 3 * cols :]
    expander_grad, reducer_grad = lax.psum((expander_part, reducer_part), "dp")
    threshold_grad, intercepts_grad = lax.psum((threshold_part, bias_part.reshape(3, cols)), "dp")
    small = jnp.stack([stretch_part, uplift_part, amplify_part, displace_part, offset_part, residue_part])
    small = lax.psum(small, ("dp", "tensor"))
    relative_grad = lax.psum(rel_part, ("dp", "tensor")).astype(F32)
    return (final.astype(BF16), tokens_grad, projector_grad, intercepts_grad, combiner_grad, small[4], relative_grad,
            small[0], small[1], expander_grad.astype(F32), threshold_grad, reducer_grad.astype(F32), small[5], small[2], small[3])


def solution(mesh):
    both = P(("dp", "tensor"), None)
    return jax.shard_map(
        shards,
        mesh=mesh,
        in_specs=(both, both, P(("dp", "tensor")), P(), P(None, "dp", "tensor"), P(None, "tensor"), P("dp", "tensor"), P(), P(), P(), P(),
                  P(None, "tensor"), P("tensor"), P("tensor", None), P(), P(), P()),
        out_specs=(both, both, P(None, "dp", "tensor"), P(None, "tensor"), P("dp", "tensor"), P(), P(), P(), P(),
                   P(None, "tensor"), P("tensor"), P("tensor", None), P(), P(), P()),
        check_vma=False,
    )
```

time: 1040 us -> 543 us (0.52)
  local copies, waits for them, and re-layouts: 315 us -> 8.64 us
  waiting for transfers between devices: 449 us -> 350 us
  blocking collectives: 167 us -> 96 us
  matrix products: 56.7 us -> 14.6 us
  Pallas kernels: 0 us -> 35.7 us
    psum x2, waiting for transfers between devices: 308 us -> 174 us  [the longest x1 109 us: shards(): expander_grad, reducer_grad = lax.psum((expander_part, reducer_part), 'dp')]
    unnamed x148 -> x60, local copies, waits for them, and re-layouts: 122 us -> 1.76 us
    reshape x8 -> x3, local copies, waits for them, and re-layouts: 77.5 us -> 2.47 us  [the longest x1 1.34 us: shards(): bias = intercepts.reshape(1, 3 * cols)]
    all_gather x6 -> x5, blocking collectives: 103 us -> 36.5 us  [the longest x1 10.5 us: shards(): x = lax.all_gather(tokens, 'tensor', axis=0, tiled=True)]
    dot_general x29 -> x10, matrix products: 56.7 us -> 14.6 us  [the longest x3 6.02 us: tn(): lax.dot_general(a, b, (((0,), (0,)), ((), ())), preferred_element_type=F32)]
    pallas_call x0 -> x2, Pallas kernels: none -> 35.7 us  [the longest x1 21.1 us: attn_bwd(): pl.pallas_call(functools.partial(attn_bwd_kernel, scale), out_shape=(S((w...]
    rev x4 -> x0, local copies, waits for them, and re-layouts: 35 us -> none  [skew(): flat = spread[:, :, ::-1].reshape(heads, length * width)]
    gather x2 -> x0, local copies, waits for them, and re-layouts: 31.1 us -> none  [the longest x1 15.6 us: assemble(): far = skew(jnp.take(far_raw, buckets, axis=2))]
  transfers between devices with their start and end apart: 8 -> 8, of which waited for: 7 -> 8; matrix products, arithmetic and copies ran while one was open for 2% -> 4% of each run, Pallas kernels for 0% -> 0%
where the time goes in v1:
time: 543 us
  waiting for transfers between devices  350 us (64%)
  blocking collectives  96 us (18%)
  Pallas kernels  35.7 us (7%)
  other arithmetic  23 us (4%)
  matrix products  14.6 us (3%)
  between operations  14.6 us (3%)
  local copies, waits for them, and re-layouts  8.64 us (2%)
    psum x1, waiting for transfers between devices, shards(): expander_grad, reducer_grad = lax.psum((expander_part, reducer_part), 'dp')  109 us
    reduce_scatter x1, waiting for transfers between devices, shards(): lax.psum_scatter(grads, 'dp', scatter_dimension=0, tiled=True).astype(F32)  66.4 us
    psum x1, waiting for transfers between devices, shards(): relative_grad = lax.psum(rel_part, ('dp', 'tensor')).astype(F32)  64.3 us
    psum x1, blocking collectives, shards(): small = lax.psum(small, ('dp', 'tensor'))  37.1 us
    all_gather x1, waiting for transfers between devices, shards(): w = lax.all_gather(packed, 'dp', axis=0, tiled=True)  30.9 us
    psum x1, blocking collectives, shards(): lax.psum((threshold_part, bias_part.reshape(3, cols)), 'dp')  22.4 us
    reduce_scatter x1, waiting for transfers between devices, shards(): lax.psum_scatter(part, 'tensor', scatter_dimension=0, tiled=True)  21.9 us
    pallas_call x1, Pallas kernels, attn_bwd(): pl.pallas_call(functools.partial(attn_bwd_kernel, scale), out_shape=(S((w...  21.1 us
  transfers between devices with their start and end apart: 8, of which 8 were waited for; matrix products, arithmetic and copies ran while one was open for 4% of the time, Pallas kernels for 0%

profile of v1, /device:TPU:0, one launch (start us, length us, event | category | flops | bytes accessed | tf_op | source)
XLA Modules:
  0.0 542.5 jit_solution(18279697794876229973)
XLA Ops:
  8.2 1.6 pad_maximum_fusion.1
  9.9 1.3 reshape.113.bias_ref
  13.2 10.5 %all_gather.18.x_ref = bf16[512,768]{1,0:T(8,128)(2,1)} all-gather(bf16[128,768]{1,0:T(8,128)(2,1)S(1)} %copy-done.1), channel_id=1, replica_groups=mesh['dp'=8,'tensor'=4] {'tensor'}, dimensions={0}, use_global_device_ids=true | all-gather | bytes 983040 | tf_op jit(solution)/shard_map/all_gather | solution.py:210
  23.7 30.9 %all-gather.3.cloned.1.call-done.w_ref = bf16[768,768]{1,0:T(8,128)(2,1)} async-done(((bf16[96,768]{1,0:T(8,128)(2,1)}), bf16[768,768]{1,0:T(8,128)(2,1)}) %all-gather.3.cloned.1.call-update) | async-done | bytes 1179664 | tf_op jit(solution)/shard_map/all_gather | solution.py:212
  54.6 14.5 %attn_fwd.1 = (f32[3,512,512]{2,1,0:T(8,128)}, bf16[512,576]{1,0:T(8,128)(2,1)}, bf16[1024,384]{1,0:T(8,128)(2,1)}, bf16[512,192]{1,0:T(8,128)(2,1)}, bf16[512,768]{1,0:T(8,128)(2,1)}) custom-call(bf16[512,768]{1,0:T(8,128)(2,1)} %all_gather.18.x_ref, bf16[768,768]{1,0:T(8,128)(2,1)} %all-gather.3.cloned.1.call-done.w_ref, ...), custom_call_target="tpu_custom_call" | custom-call | tf_op jit(solution)/shard_map/attn_fwd/pallas_call | solution.py:76
  69.3 21.9 %reduce-scatter.6.cloned.1.call-done = bf16[128,768]{1,0:T(8,128)(2,1)} async-done(((bf16[512,768]{1,0:T(8,128)(2,1)}), bf16[128,768]{1,0:T(8,128)(2,1)}) %reduce-scatter.6.cloned.1.call-update) | async-done | bytes 196624 | tf_op jit(solution)/shard_map/reduce_scatter | solution.py:222
  94.6 8.0 %all_gather.20 = bf16[512,768]{1,0:T(8,128)(2,1)S(1)} all-gather(bf16[128,768]{1,0:T(8,128)(2,1)S(1)} %fusion.12), channel_id=1, replica_groups=mesh['dp'=8,'tensor'=4] {'tensor'}, dimensions={0}, use_global_device_ids=true | all-gather | bytes 983040 | tf_op jit(solution)/shard_map/all_gather | solution.py:224
  102.6 3.7 convolution_convert_fusion.2
  106.4 5.1 all-gather
  113.2 17.0 %reduce-scatter.8.cloned.1.call-done = bf16[128,768]{1,0:T(8,128)(2,1)} async-done(((bf16[512,768]{1,0:T(8,128)(2,1)}), bf16[128,768]{1,0:T(8,128)(2,1)}) %reduce-scatter.8.cloned.1.call-update) | async-done | bytes 196624 | tf_op jit(solution)/shard_map/reduce_scatter | solution.py:229
  130.2 1.2 fusion.32
  132.5 2.3 convert_reduce_fusion.1
  135.6 6.1 %all_gather.22 = bf16[256,768]{1,0:T(8,128)(2,1)S(1)} all-gather(bf16[64,768]{1,0:T(8,128)(2,1)S(1)} %convolution_convert_fusion.6), channel_id=1, replica_groups=mesh['dp'=8,'tensor'=4] {'tensor'}, dimensions={0}, use_global_device_ids=true | all-gather | bytes 491520 | tf_op jit(solution)/shard_map/all_gather | solution.py:235
  143.8 1.2 convolution_convert_fusion.3
  145.7 1.3 eq.42
  147.0 1.4 fusion.16.sel_ref
  148.4 17.9 %reduce-scatter.10.cloned.1.call-done = bf16[64,768]{1,0:T(8,128)(2,1)} async-done(((bf16[256,768]{1,0:T(8,128)(2,1)}), bf16[64,768]{1,0:T(8,128)(2,1)}) %reduce-scatter.10.cloned.1.call-update) | async-done | bytes 98320 | tf_op jit(solution)/shard_map/reduce_scatter | solution.py:247
  166.3 1.9 multiply_reduce_fusion.1
  169.9 6.8 %all_gather.23.rows_ref = bf16[256,768]{1,0:T(8,128)(2,1)} all-gather(bf16[64,768]{1,0:T(8,128)(2,1)S(1)} %convolution_convert_fusion.5), channel_id=1, replica_groups=mesh['dp'=8,'tensor'=4] {'tensor'}, dimensions={0}, use_global_device_ids=true | all-gather | bytes 491520 | tf_op jit(solution)/shard_map/all_gather | solution.py:252
  176.7 21.1 %attn_bwd.1 = (bf16[768,768]{1,0:T(8,128)(2,1)}, bf16[512,768]{1,0:T(8,128)(2,1)}, bf16[512,768]{1,0:T(8,128)(2,1)}, f32[1,576]{1,0:T(1,128)}) custom-call(bf16[512,768]{1,0:T(8,128)(2,1)} %all_gather.18.x_ref, bf16[768,768]{1,0:T(8,128)(2,1)} %all-gather.3.cloned.1.call-done.w_ref, bf16[512,768]{1,0:T(8,128)(2,1)} %rel_ref.3, s32[1024,1]{1,0:T(8,128)} %copy.34.bcol_ref, ...), custom_call_target="tpu_custom_call" | custom-call | tf_op jit(solution)/shard_map/attn_bwd/pallas_call | solution.py:170
  197.9 2.5 convolution_convert_fusion.1
  200.4 1.6 convolution_convert_fusion
  203.9 22.4 %all-reduce = (f32[3,192]{1,0:T(4,128)}, f32[768]{0:T(1024)}) all-reduce(f32[3,192]{1,0:T(4,128)S(1)} %reshape.117, f32[768]{0:T(1024)S(1)} %copy-done.21), channel_id=1, replica_groups=mesh['dp'=8,'tensor'=4] {'dp'}, use_global_device_ids=true, to_apply=%region_14.15 | all-reduce | flops 1344 | bytes 10752 | tf_op jit(solution)/shard_map/psum | solution.py:259
  226.3 37.1 %psum.43 = f32[6,768]{1,0:T(8,128)S(1)} all-reduce(f32[6,768]{1,0:T(8,128)S(1)} %stack.43), channel_id=1, replica_groups=mesh['dp'=8,'tensor'=4] {'dp','tensor'}, use_global_device_ids=true, to_apply=%region_21.22 | all-reduce | flops 4608 | bytes 36864 | tf_op jit(solution)/shard_map/psum | solution.py:261
  264.0 64.3 %all-reduce.5.cloned.1.call-done = bf16[512,768]{1,0:T(8,128)(2,1)} async-done(((bf16[512,768]{1,0:T(8,128)(2,1)}), bf16[512,768]{1,0:T(8,128)(2,1)}) %all-reduce.5.cloned.1.call-update) | async-done | bytes 786448 | tf_op jit(solution)/shard_map/psum | solution.py:262
  328.3 2.4 convert_element_type.118
  330.7 109.3 %all-reduce.7.cloned.1.call-done = (bf16[768,768]{1,0:T(8,128)(2,1)}, bf16[768,768]{1,0:T(8,128)(2,1)}) async-done(((bf16[768,768]{1,0:T(8,128)(2,1)}, bf16[768,768]{1,0:T(8,128)(2,1)}), (bf16[768,768]{1,0:T(8,128)(2,1)}, bf16[768,768]{1,0:T(8,128)(2,1)})) %all-reduce.7.cloned.1.call-update) | async-done | bytes 2359312 | tf_op jit(solution)/shard_map/psum | solution.py:258
  440.1 2.9 convert_element_type.120
  443.0 1.6 convert_element_type.124
  444.6 20.4 %reduce-scatter.12.cloned.1.call-done = bf16[128,768]{1,0:T(8,128)(2,1)} async-done(((bf16[512,768]{1,0:T(8,128)(2,1)}), bf16[128,768]{1,0:T(8,128)(2,1)}) %reduce-scatter.12.cloned.1.call-update) | async-done | bytes 196624 | tf_op jit(solution)/shard_map/reduce_scatter | solution.py:254
  465.0 1.7 convert_add_fusion
  466.7 66.4 %reduce-scatter.14.cloned.1.call-done = bf16[96,768]{1,0:T(8,128)(2,1)} async-done(((bf16[768,768]{1,0:T(8,128)(2,1)}), bf16[96,768]{1,0:T(8,128)(2,1)}) %reduce-scatter.14.cloned.1.call-update) | async-done | bytes 147472 | tf_op jit(solution)/shard_map/reduce_scatter | solution.py:255
  (120 shorter events, 19.4 us)
Async XLA Ops:
  7.2 95.4 %copy-start = (bf16[768,768]{1,0:T(8,128)(2,1)S(1)}, bf16[768,768]{1,0:T(8,128)(2,1)}, u32[]{:S(2)}) copy-start(bf16[768,768]{1,0:T(8,128)(2,1)} %param.28) | copy-start | bytes 3538948
  7.2 6.0 %copy-start.1 = (bf16[128,768]{1,0:T(8,128)(2,1)S(1)}, bf16[128,768]{1,0:T(8,128)(2,1)}, u32[]{:S(2)}) copy-start(bf16[128,768]{1,0:T(8,128)(2,1)} %param.17) | copy-start | bytes 589828
  7.2 47.4 %all-gather.3.cloned.1.call-start = ((), (), s32[]{:S(2)}) async-start(), calls=%async_computation.5 | async-start | bytes 1327104 | tf_op jit(solution)/shard_map/all_gather | solution.py:212
  9.8 81.4 %reduce-scatter.6.cloned.1.call-start = ((), (), s32[]{:S(2)}) async-start(), calls=%async_computation.6 | async-start | bytes 983040 | tf_op jit(solution)/shard_map/reduce_scatter | solution.py:222
  23.7 45.6 %copy-start.23 = (bf16[768]{0:T(1024)(128)(2,1)S(1)}, bf16[768]{0:T(1024)(128)(2,1)}, u32[]{:S(2)}) copy-start(bf16[768]{0:T(1024)(128)(2,1)} %param.24) | copy-start | bytes 4612
  23.7 45.6 %copy-start.24 = (bf16[768]{0:T(1024)(128)(2,1)S(1)}, bf16[768]{0:T(1024)(128)(2,1)}, u32[]{:S(2)}) copy-start(bf16[768]{0:T(1024)(128)(2,1)} %param.29) | copy-start | bytes 4612
  69.2 24.3 %copy-start.8 = (f32[768]{0:T(1024)S(1)}, f32[768]{0:T(1024)}, u32[]{:S(2)}) copy-start(f32[768]{0:T(1024)} %param.26) | copy-start | bytes 9220
  69.2 24.3 %copy-start.9 = (f32[768]{0:T(1024)S(1)}, f32[768]{0:T(1024)}, u32[]{:S(2)}) copy-start(f32[768]{0:T(1024)} %param.27) | copy-start | bytes 9220
  69.2 61.0 %reduce-scatter.8.cloned.1.call-start = ((), (), s32[]{:S(2)}) async-start(), calls=%async_computation.7 | async-start | bytes 983040 | tf_op jit(solution)/shard_map/reduce_scatter | solution.py:229
  92.3 37.9 %copy-start.14 = (f32[128]{0:T(128)}, f32[128]{0:T(128)S(1)}, u32[]{:S(2)}) copy-start(f32[128]{0:T(128)S(1)} %broadcast_multiply_fusion.5) | copy-start | bytes 1540
  93.5 36.7 %copy-start.17 = (f32[128]{0:T(128)}, f32[128]{0:T(128)S(1)}, u32[]{:S(2)}) copy-start(f32[128]{0:T(128)S(1)} %add_rsqrt_fusion.1) | copy-start | bytes 1540
  102.6 3.8 copy-start.27
  102.6 9.2 %copy-start.25 = (bf16[768]{0:T(1024)(128)(2,1)S(1)}, bf16[768]{0:T(1024)(128)(2,1)}, u32[]{:S(2)}) copy-start(bf16[768]{0:T(1024)(128)(2,1)} %param.31) | copy-start | bytes 4612
  106.3 59.9 %reduce-scatter.10.cloned.1.call-start = ((), (), s32[]{:S(2)}) async-start(), calls=%async_computation.8 | async-start | bytes 491520 | tf_op jit(solution)/shard_map/reduce_scatter | solution.py:247
  106.4 25.3 %copy-start.26 = (f32[128]{0:T(128)}, f32[128]{0:T(128)S(1)}, u32[]{:S(2)}) copy-start(f32[128]{0:T(128)S(1)} %convert_element_type.105) | copy-start | bytes 1540
  112.7 17.5 %copy-start.2 = (bf16[128,768]{1,0:T(8,128)(2,1)S(1)}, bf16[128,768]{1,0:T(8,128)(2,1)}, u32[]{:S(2)}) copy-start(bf16[128,768]{1,0:T(8,128)(2,1)} %reduce-scatter.6.cloned.1.call-done) | copy-start | bytes 589828
  113.2 18.5 %copy-start.5 = (bf16[128,768]{1,0:T(8,128)(2,1)S(1)}, bf16[128,768]{1,0:T(8,128)(2,1)}, u32[]{:S(2)}) copy-start(bf16[128,768]{1,0:T(8,128)(2,1)} %param.18) | copy-start | bytes 589828
  113.2 18.5 %copy-start.10 = (f32[768]{0:T(1024)S(1)}, f32[768]{0:T(1024)}, u32[]{:S(2)}) copy-start(f32[768]{0:T(1024)} %param.32) | copy-start | bytes 9220
  130.2 2.3 copy-start.6
  130.2 2.3 copy-start.18
  132.5 9.3 %copy-start.28 = (bf16[768,768]{1,0:T(8,128)(2,1)S(1)}, bf16[768,768]{1,0:T(8,128)(2,1)}, u32[]{:S(2)}) copy-start(bf16[768,768]{1,0:T(8,128)(2,1)} %param.30) | copy-start | bytes 3538948
  143.8 22.5 %copy-start.15 = (f32[128]{0:T(128)S(1)}, f32[128]{0:T(128)}, u32[]{:S(2)}) copy-start(f32[128]{0:T(128)} %copy-done.14) | copy-start | bytes 1540
  145.0 183.3 %all-reduce.5.cloned.1.call-start = ((), (), s32[]{:S(2)}) async-start(), calls=%async_computation.11 | async-start | bytes 1572864 | tf_op jit(solution)/shard_map/psum | solution.py:262
  197.8 242.2 %all-reduce.7.cloned.1.call-start = ((), (), s32[]{:S(2)}) async-start(), calls=%async_computation.12 | async-start | bytes 4718592 | tf_op jit(solution)/shard_map/psum | solution.py:258
  202.1 1.6 copy-start.20
  202.1 1.6 copy-start.19
  202.1 1.7 copy-start.22
  202.1 1.8 copy-start.21
  202.1 262.9 %reduce-scatter.12.cloned.1.call-start = ((), (), s32[]{:S(2)}) async-start(), calls=%async_computation.9 | async-start | bytes 983040 | tf_op jit(solution)/shard_map/reduce_scatter | solution.py:254
  202.9 330.2 %reduce-scatter.14.cloned.1.call-start = ((), (), s32[]{:S(2)}) async-start(), calls=%async_computation.10 | async-start | bytes 1327104 | tf_op jit(solution)/shard_map/reduce_scatter | solution.py:255
  440.1 2.9 copy-start.4
  533.1 1.8 copy-start.7
  (5 other events, 7.0 us)
Sparse Core Ops, SparseCore 0:
  10.8 43.8 all-gather.2
  69.3 21.8 reduce-scatter.5
  106.4 23.7 reduce-scatter.7
  145.2 21.0 reduce-scatter.9
  197.9 130.3 all-reduce.4
  332.4 107.6 all-reduce.6
  442.6 22.3 reduce-scatter.11
  468.4 64.6 reduce-scatter.13

commit v2 on v1

v2 whole, which is shorter than its diff:
```python
import functools
import math

import jax, jax.numpy as jnp
from jax import lax
from jax.experimental import pallas as pl
from jax.experimental.pallas import tpu as pltpu
from jax.sharding import PartitionSpec as P

HEAD_DIM = 64
BLK = 128
EPSILON = 1e-05
F32, BF16 = jnp.float32, jnp.bfloat16

def nn(a, b):
    return lax.dot_general(a, b, (((1,), (0,)), ((), ())), preferred_element_type=F32)

def nt(a, b):
    return lax.dot_general(a, b, (((1,), (1,)), ((), ())), preferred_element_type=F32)

def tn(a, b):
    return lax.dot_general(a, b, (((0,), (0,)), ((), ())), preferred_element_type=F32)

def attn_fwd_kernel(scale, x_ref, w_ref, bias_ref, rel_ref, bcol_ref, chosen_ref,
                    probs_ref, mixed_ref, table_ref, ctx_ref, part_ref, sel_ref, far_ref, acc_ref):
    length = x_ref.shape[0]
    cols = ctx_ref.shape[1]
    classes = rel_ref.shape[0]
    span = table_ref.shape[0]
    blocks = length // BLK
    win = length + BLK
    bias = bias_ref[...].astype(F32)
    mixed_ref[...] = (nn(x_ref[...], w_ref[:, : 3 * cols]) + bias).astype(BF16)
    pos = (nn(rel_ref[...], w_ref[:, : 2 * cols]) + bias[:, : 2 * cols]).astype(BF16)
    spread = (bcol_ref[...] == lax.broadcasted_iota(jnp.int32, (span, classes), 1)).astype(BF16)
    table_ref[...] = nn(spread, pos).astype(BF16)
    quarter = chosen_ref.shape[2]
    below = (lax.broadcasted_iota(jnp.int32, (quarter, quarter), 0) <= lax.broadcasted_iota(jnp.int32, (quarter, quarter), 1)).astype(BF16)
    order = lax.broadcasted_iota(jnp.int32, sel_ref.shape[1:], 0).astype(F32) + 1.0
    for q in range(sel_ref.shape[0]):
        rank = nn(chosen_ref[q].astype(BF16), below)[:1]
        sel_ref[q] = jnp.where(rank == order, chosen_ref[q, :1], 0.0).astype(BF16)
    lanes = lax.broadcasted_iota(jnp.int32, (1, cols), 1) // HEAD_DIM
    acc_ref[...] = jnp.zeros_like(acc_ref)

    def head(h, carry):
        own = lanes == h
        pick = lambda v: jnp.where(own, v, jnp.zeros_like(v))
        key_h = pick(mixed_ref[:, cols : 2 * cols])
        for b in range(blocks):
            start = length - BLK * (b + 1)
            rows = slice(BLK * b, BLK * (b + 1))
            wide = nt(key_h[rows], table_ref[start : start + win, :cols])
            turned = pltpu.roll(wide, win - BLK + 1, 1, stride=1, stride_axis=0)[:, :length]
            far_ref[:, rows] = turned.T
        value_h = pick(mixed_ref[:, 2 * cols : 3 * cols])
        for b in range(blocks):
            start = length - BLK * (b + 1)
            rows = slice(BLK * b, BLK * (b + 1))
            query = pick(mixed_ref[rows, :cols])
            wide = nt(query, table_ref[start : start + win, cols : 2 * cols])
            near = pltpu.roll(wide, win - BLK + 1, 1, stride=1, stride_axis=0)[:, :length]
            scores = (nt(query, key_h) + near + far_ref[rows, :]) * scale
            top = jnp.max(scores, -1, keepdims=True)
            weights = jnp.exp(scores - top)
            probs = weights / jnp.sum(weights, -1, keepdims=True)
            probs_ref[h, rows, :] = probs
            acc_ref[rows, :] += nn(probs.astype(BF16), value_h)
        return carry

    lax.fori_loop(0, cols // HEAD_DIM, head, 0)
    ctx_ref[...] = acc_ref[...].astype(BF16)
    part_ref[...] = nt(ctx_ref[...], w_ref[:, 3 * cols :]).astype(BF16)

def attn_fwd(x, w, bias, rel, bcol, chosen, keep):
    length = x.shape[0]
    cols = w.shape[1] // 4
    width = w.shape[0]
    scale = 1.0 / math.sqrt(3 * HEAD_DIM)
    heads = cols // HEAD_DIM
    span = bcol.shape[0]
    S = jax.ShapeDtypeStruct
    return pl.pallas_call(
        functools.partial(attn_fwd_kernel, scale),
        out_shape=(S((heads, length, length), F32), S((length, 3 * cols), BF16), S((span, 2 * cols), BF16),
                   S((length, cols), BF16), S((length, width), BF16), S((chosen.shape[0], keep, chosen.shape[2]), BF16)),
        scratch_shapes=[pltpu.VMEM((length, length), F32), pltpu.VMEM((length, cols), F32)],
        name="attn_fwd",
    )(x, w, bias, rel, bcol, chosen)

def attn_bwd_kernel(scale, x_ref, w_ref, rel_ref, bcol_ref, probs_ref, mixed_ref, table_ref, ctx_ref, rows_ref, sel_ref, past_ref, thr_ref,
                    grads_ref, part_ref, relpart_ref, small_ref,
                    dctx_ref, dctx_t, turn_t, dq_ref, dk_ref, dv_t, dpos_t, ds_ref):
    length = x_ref.shape[0]
    cols = ctx_ref.shape[1]
    classes = rel_ref.shape[0]
    span = table_ref.shape[0]
    blocks = length // BLK
    win = length + BLK
    keep = sel_ref.shape[1]
    flip = (lax.broadcasted_iota(jnp.int32, (BLK, BLK), 0) + lax.broadcasted_iota(jnp.int32, (BLK, BLK), 1) == BLK - 1).astype(BF16)
    small = nn(rows_ref[...], w_ref[:, 3 * cols :]).astype(BF16)
    ctx_small = []
    for b in range(blocks):
        rows = slice(BLK * b, BLK * (b + 1))
        few = slice(keep * b, keep * (b + 1))
        dctx_ref[rows, :] = tn(sel_ref[b], small[few]).astype(BF16)
        ctx_small.append(nn(sel_ref[b], ctx_ref[rows, :]).astype(BF16))
        turn_t[:cols, rows] = tn(mixed_ref[rows, :cols], flip).astype(BF16)
        turn_t[cols:, rows] = tn(mixed_ref[rows, cols : 2 * cols], flip).astype(BF16)
    dctx_t[...] = dctx_ref[...].T
    grads_ref[:, 3 * cols :] = tn(rows_ref[...], jnp.concatenate(ctx_small, 0)).astype(BF16)
    lanes = lax.broadcasted_iota(jnp.int32, (1, cols), 1) // HEAD_DIM
    dq_ref[...] = jnp.zeros_like(dq_ref)
    dk_ref[...] = jnp.zeros_like(dk_ref)
    dpos_t[...] = jnp.zeros_like(dpos_t)
    blank = jnp.zeros((BLK, BLK), F32)

    def head(h, carry):
        own = lanes == h
        pick = lambda v: jnp.where(own, v, jnp.zeros_like(v))
        mine = pl.ds(pl.multiple_of(h * HEAD_DIM, HEAD_DIM), HEAD_DIM)
        key_h = pick(mixed_ref[:, cols : 2 * cols])
        query_h = pick(mixed_ref[:, :cols])
        value = mixed_ref[:, 2 * cols : 3 * cols]
        posq_h = pick(table_ref[:, :cols])
        posk_h = pick(table_ref[:, cols : 2 * cols])
        total = jnp.zeros((HEAD_DIM, length), F32)
        for b in range(blocks):
            start = length - BLK * (b + 1)
            rows = slice(BLK * b, BLK * (b + 1))
            probs = probs_ref[h, rows, :]
            dprobs = nt(pick(dctx_ref[rows, :]), value)
            dscores = (probs * (dprobs - jnp.sum(probs * dprobs, -1, keepdims=True))).astype(BF16)
            ds_ref[rows, :] = dscores
            total += nn(dctx_t[mine, rows], probs.astype(BF16))
            turned = nn(flip, dscores)
            moved = pltpu.roll(jnp.concatenate([turned, blank], 1), 0, 1, stride=1, stride_axis=0).astype(BF16)
            dq_ref[rows, :] += nn(turned.astype(BF16), key_h) + nn(moved, posk_h[start : start + win])
            low = pl.ds(pl.multiple_of(cols + h * HEAD_DIM, HEAD_DIM), HEAD_DIM)
            dpos_t[low, start : start + win] += nn(turn_t[mine, rows], moved)
        dv_t[mine, :] = total
        for b in range(blocks):
            start = length - BLK * (b + 1)
            rows = slice(BLK * b, BLK * (b + 1))
            turned = nt(flip, ds_ref[:, rows])
            moved = pltpu.roll(jnp.concatenate([turned, blank], 1), 0, 1, stride=1, stride_axis=0).astype(BF16)
            dk_ref[rows, :] += nn(turned.astype(BF16), query_h) + nn(moved, posq_h[start : start + win])
            low = pl.ds(pl.multiple_of(cols + h * HEAD_DIM, HEAD_DIM), HEAD_DIM)
            dpos_t[mine, start : start + win] += nn(turn_t[low, rows], moved)
        return carry

    lax.fori_loop(0, cols // HEAD_DIM, head, 0)
    order = lambda ref: jnp.concatenate([nn(flip, (ref[BLK * b : BLK * (b + 1), :] * scale).astype(BF16)).astype(BF16) for b in range(blocks)], 0)
    dmixed = jnp.concatenate([order(dq_ref), order(dk_ref), dv_t[...].T.astype(BF16)], 1)
    spread = (bcol_ref[...] == lax.broadcasted_iota(jnp.int32, (span, classes), 1)).astype(BF16)
    wide = dpos_t[...] * scale
    high = wide.astype(BF16)
    dpos = (nn(high, spread) + nn((wide - high.astype(F32)).astype(BF16), spread)).T
    dpos_low = dpos.astype(BF16)
    sums = jnp.sum(dmixed.astype(F32), 0, keepdims=True)
    small_ref[...] = past_ref[...]
    small_ref[THRESHOLD : THRESHOLD + 1, :] = thr_ref[...]
    small_ref[BIAS : BIAS + 1, : 2 * cols] = sums[:, : 2 * cols] + jnp.sum(dpos, 0, keepdims=True)
    small_ref[BIAS : BIAS + 1, 2 * cols : 3 * cols] = sums[:, 2 * cols :]
    relpart_ref[...] = nt(dpos_low, w_ref[:, : 2 * cols]).astype(BF16)
    part_ref[...] = nt(dmixed, w_ref[:, : 3 * cols]).astype(BF16)
    both = tn(x_ref[...], dmixed)
    grads_ref[:, : 2 * cols] = (both[:, : 2 * cols] + tn(rel_ref[...], dpos_low)).astype(BF16)
    grads_ref[:, 2 * cols : 3 * cols] = both[:, 2 * cols :].astype(BF16)

def attn_bwd(x, w, rel, bcol, probs, mixed, table, ctx, rows, sel, past, thr):
    length, width = x.shape
    cols = w.shape[1] // 4
    scale = 1.0 / math.sqrt(3 * HEAD_DIM)
    span = bcol.shape[0]
    S = jax.ShapeDtypeStruct
    V = pltpu.VMEM
    return pl.pallas_call(
        functools.partial(attn_bwd_kernel, scale),
        out_shape=(S((width, 4 * cols), BF16), S((length, width), BF16), S((rel.shape[0], width), BF16), S(past.shape, F32)),
        scratch_shapes=[V((length, cols), BF16), V((cols, length), BF16), V((2 * cols, length), BF16), V((length, cols), F32), V((length, cols), F32),
                        V((cols, length), F32), V((2 * cols, span), F32), V((length, length), BF16)],
        name="attn_bwd",
    )(x, w, rel, bcol, probs, mixed, table, ctx, rows, sel, past, thr)


MESH = pl.DeviceIdType.MESH


def at_place(spot, n):
    return jnp.where(spot < n // 2, 2 * spot, 2 * (n - 1 - spot) + 1)


def place_of(index, n):
    return jnp.where(index % 2 == 0, index // 2, n - 1 - index // 2)


class Links:
    def __init__(self, n):
        self.n = n
        self.dp = lax.axis_index("dp")
        self.me = lax.axis_index("tensor")
        self.spot = place_of(self.dp, n)
        self.right = (at_place((self.spot + 1) % n, n), self.me)
        self.left = (at_place((self.spot + n - 1) % n, n), self.me)
        self.core = self.me % 2
        self.twin = (self.dp, self.me + 1 - 2 * self.core)
        self.across = (self.dp, (self.me + 2) % 4)

    def chunk(self, shift):
        return at_place((self.spot + shift + 2 * self.n) % self.n, self.n)

    def greet(self, ring, pair):
        peers = ([self.left, self.right] if ring else []) + ([self.twin, self.across] if pair else [])
        barrier = pltpu.get_barrier_semaphore()
        for peer in peers:
            pl.semaphore_signal(barrier, inc=1, device_id=peer, device_id_type=MESH)
        pl.semaphore_wait(barrier, len(peers))


class Sems:
    def __init__(self, send, recv):
        self.send, self.recv, self.used = send, recv, 0

    def copy(self, src, dst, peer):
        k = self.used
        self.used += 1
        return pltpu.make_async_remote_copy(src_ref=src, dst_ref=dst, send_sem=self.send.at[k], recv_sem=self.recv.at[k],
                                            device_id=peer, device_id_type=MESH)


def run_all(*tasks):
    tasks = list(tasks)
    while tasks:
        for task in list(tasks):
            try:
                next(task)
            except StopIteration:
                tasks.remove(task)


def ring_gather(links, sems, full, own=None):
    n = links.n
    half = n // 2
    cut = full.shape[2] // 2
    sides = ((links.right, -1, slice(0, cut)), (links.left, 1, slice(cut, 2 * cut)))
    made = []
    for s in range(half):
        last = s == half - 1
        for k, (peer, step, part) in enumerate(sides):
            if s:
                made[2 * (s - 1) + k].wait_recv()
            index = links.chunk(step * s)
            dst = full.at[index, :, part] if last else full.at[index]
            src = dst if s or own is None else (own.at[:, part] if last else own)
            made.append(sems.copy(src, dst, peer))
            made[-1].start()
        yield
    for k in range(2):
        made[2 * (half - 1) + k].wait_recv()
    for copy in made:
        copy.wait_send()


def ring_scatter(links, sems, parts, slots, done):
    n = links.n
    half = n // 2
    cut = parts.shape[2] // 2
    sides = ((links.right, 1, slice(0, cut), slice(cut, 2 * cut)), (links.left, -1, slice(cut, 2 * cut), slice(0, cut)))
    made = []
    for s in range(half):
        for k, (peer, step, part, rest) in enumerate(sides):
            index = links.chunk(step * (half - s))
            if s == 0:
                src, dst = parts.at[index, :, part], slots.at[k, 0, :, part]
            else:
                made[2 * (s - 1) + k].wait_recv()
                held = slots.at[k, s - 1]
                if s == 1:
                    held[:, part] = (held[:, part].astype(F32) + parts[index, :, part].astype(F32)).astype(BF16)
                    held[:, rest] = parts[index, :, rest]
                else:
                    held[...] = (held[...].astype(F32) + parts[index].astype(F32)).astype(BF16)
                src, dst = held, slots.at[k, s]
            made.append(sems.copy(src, dst, peer))
            made[-1].start()
        yield
    for k in range(2):
        made[2 * (half - 1) + k].wait_recv()
    done(parts[links.dp].astype(F32) + slots[0, half - 1].astype(F32) + slots[1, half - 1].astype(F32))
    for copy in made:
        copy.wait_send()


def group_gather(links, sems, full, own=None):
    mine = full.at[links.me]
    src = mine if own is None else own
    over = sems.copy(src, mine, links.across)
    over.start()
    near = sems.copy(src, mine, links.twin)
    near.start()
    yield
    over.wait_recv()
    block = full.at[(links.me + 2) % 4]
    on = sems.copy(block, block, links.twin)
    on.start()
    yield
    near.wait_recv()
    on.wait_recv()
    for copy in (over, near, on):
        copy.wait_send()


def group_scatter(links, sems, parts, slots, done):
    mine, other = links.me, (links.me + 2) % 4
    twin = links.me + 1 - 2 * links.core
    first = sems.copy(parts.at[(twin + 2) % 4], slots.at[0], links.twin)
    first.start()
    second = sems.copy(parts.at[twin], slots.at[1], links.twin)
    second.start()
    yield
    first.wait_recv()
    slots[0] = (slots[0].astype(F32) + parts[other].astype(F32)).astype(BF16)
    over = sems.copy(slots.at[0], slots.at[2], links.across)
    over.start()
    yield
    second.wait_recv()
    over.wait_recv()
    done(parts[mine].astype(F32) + slots[1].astype(F32) + slots[2].astype(F32))
    for copy in (first, second, over):
        copy.wait_send()


def comm_call(kernel, ident, outs, scratch, sems, args, name):
    return pl.pallas_call(
        kernel,
        out_shape=outs,
        scratch_shapes=list(scratch) + [pltpu.SemaphoreType.DMA((sems,)), pltpu.SemaphoreType.DMA((sems,))],
        compiler_params=pltpu.CompilerParams(collective_id=ident, has_side_effects=True),
        name=name,
    )(*args)


def normalize(value, gain, shift):
    mean = jnp.mean(value, -1, keepdims=True)
    center = value - mean
    inverse = lax.rsqrt(jnp.mean(center * center, -1, keepdims=True) + EPSILON)
    unit = center * inverse
    return (unit * gain + shift, unit, inverse)


def normalize_back(incoming, gain, unit, inverse):
    scaled = incoming * gain
    result = inverse * (scaled - jnp.mean(scaled, -1, keepdims=True) - unit * jnp.mean(scaled * unit, -1, keepdims=True))
    return (result, jnp.sum(incoming * unit, 0, keepdims=True), jnp.sum(incoming, 0, keepdims=True))


OFFSET, RESIDUE, STRETCH, UPLIFT, AMPLIFY, DISPLACE, THRESHOLD, BIAS = range(8)


def row(ref, k):
    return ref[k : k + 1, :]


def enter_kernel(n, tok_ref, own_ref, pick_ref, x_ref, w_ref, chosen_ref, send, recv):
    links, sems = Links(n), Sems(send, recv)
    links.greet(True, True)
    x_ref[links.me] = tok_ref[...]
    w_ref[links.dp] = own_ref[...]
    chosen_ref[links.me] = pick_ref[...]
    run_all(group_gather(links, sems, x_ref, tok_ref), ring_gather(links, sems, w_ref, own_ref), group_gather(links, sems, chosen_ref, pick_ref))


def mid_kernel(n, part_ref, tok_ref, par_ref, hidden_ref, mid_ref, unit_ref, inverse_ref, slots, send, recv):
    links, sems = Links(n), Sems(send, recv)
    links.greet(False, True)

    def done(total):
        mid, unit, inverse = normalize(tok_ref[...].astype(F32) + total + row(par_ref, OFFSET), row(par_ref, STRETCH), row(par_ref, UPLIFT))
        mid_ref[...] = mid
        unit_ref[...] = unit
        inverse_ref[...] = jnp.broadcast_to(inverse, inverse_ref.shape)
        hidden_ref[links.me] = mid.astype(BF16)

    run_all(group_scatter(links, sems, part_ref, slots, done))
    run_all(group_gather(links, sems, hidden_ref))


def end_kernel(n, part_ref, mid_ref, cot_ref, sel_ref, par_ref, result_ref, dend_ref, rows_ref, small_ref, slots, send, recv):
    links, sems = Links(n), Sems(send, recv)
    links.greet(False, True)
    mine = sel_ref[links.me]
    marks = tn(mine, jnp.ones((mine.shape[0], 128), BF16))[:, :1]

    def done(total):
        value, unit, inverse = normalize(mid_ref[...] + total + row(par_ref, RESIDUE), row(par_ref, AMPLIFY), row(par_ref, DISPLACE))
        result_ref[...] = value.astype(BF16)
        upstream = cot_ref[...].astype(F32) * marks
        d_end, gain, shift = normalize_back(upstream, row(par_ref, AMPLIFY), unit, inverse)
        dend_ref[...] = d_end
        low = d_end.astype(BF16)
        rows_ref[links.me] = nn(mine, low).astype(BF16)
        small_ref[...] = jnp.zeros_like(small_ref)
        small_ref[AMPLIFY : AMPLIFY + 1, :] = gain
        small_ref[DISPLACE : DISPLACE + 1, :] = shift
        small_ref[RESIDUE : RESIDUE + 1, :] = jnp.sum(low.astype(F32), 0, keepdims=True)

    run_all(group_scatter(links, sems, part_ref, slots, done))
    run_all(group_gather(links, sems, rows_ref))


def back_kernel(n, part_ref, dend_ref, unit_ref, inverse_ref, sel_ref, par_ref, past_ref, dmid_ref, rows_ref, small_ref, slots, send, recv):
    links, sems = Links(n), Sems(send, recv)
    links.greet(False, True)
    mine = sel_ref[links.me]

    def done(total):
        high = total.astype(BF16)
        spread = tn(mine, high) + tn(mine, (total - high.astype(F32)).astype(BF16))
        d_mid, gain, shift = normalize_back(dend_ref[...] + spread, row(par_ref, STRETCH), unit_ref[...], inverse_ref[:, :1])
        dmid_ref[...] = d_mid
        low = d_mid.astype(BF16)
        rows_ref[links.me] = nn(mine, low).astype(BF16)
        small_ref[...] = past_ref[...]
        small_ref[STRETCH : STRETCH + 1, :] = gain
        small_ref[UPLIFT : UPLIFT + 1, :] = shift
        small_ref[OFFSET : OFFSET + 1, :] = jnp.sum(low.astype(F32), 0, keepdims=True)

    run_all(group_scatter(links, sems, part_ref, slots, done))
    run_all(group_gather(links, sems, rows_ref))


def total_kernel(n, dexp_ref, dred_ref, exp_ref, red_ref, exp_slots, red_slots, send, recv):
    links, sems = Links(n), Sems(send, recv)
    links.greet(True, False)

    def total(parts, slots, full):
        def done(value):
            full[links.dp] = value.astype(BF16)

        yield from ring_scatter(links, sems, parts, slots, done)
        yield from ring_gather(links, sems, full)

    run_all(total(dexp_ref, exp_slots, exp_ref), total(dred_ref, red_slots, red_ref))


def exit_kernel(n, grads_ref, tok_ref, rel_ref, small_ref, dmid_ref, weights_ref, tokens_ref, relative_ref, sums_ref,
                grad_slots, tok_slots, rel_slots, rel_own, rel_ring, small_all, small_slots, send, recv):
    links, sems = Links(n), Sems(send, recv)
    links.greet(True, True)

    def grads_done(total):
        weights_ref[...] = total

    def tokens_done(total):
        tokens_ref[...] = dmid_ref[...] + total

    def rel_done(total):
        rel_own[...] = total.astype(BF16).reshape(rel_own.shape)

    def small():
        shared = lax.broadcasted_iota(jnp.int32, small_ref.shape, 0) < THRESHOLD
        a = sems.copy(small_ref, small_slots.at[0], links.twin)
        a.start()
        yield
        a.wait_recv()
        small_slots[1] = small_ref[...] + jnp.where(shared, small_slots[0], 0.0)
        b = sems.copy(small_slots.at[1], small_slots.at[2], links.across)
        b.start()
        yield
        b.wait_recv()
        small_all[links.dp] = small_slots[1] + jnp.where(shared, small_slots[2], 0.0)
        yield from ring_gather(links, sems, small_all)
        a.wait_send()
        b.wait_send()
        sums_ref[...] = jnp.sum(small_all[...], 0)

    def relative():
        yield from group_scatter(links, sems, rel_ref, rel_slots, rel_done)

        def own_done(total):
            place = relative_ref.at[links.me]
            place[links.dp] = total.astype(BF16)

        yield from ring_scatter(links, sems, rel_own, rel_ring, own_done)
        yield from ring_gather(links, sems, relative_ref.at[links.me])
        yield from group_gather(links, sems, relative_ref)

    run_all(relative(), small(), ring_scatter(links, sems, grads_ref, grad_slots, grads_done), group_scatter(links, sems, tok_ref, tok_slots, tokens_done))


def cumulative(inner):
    return 0.5 * (1.0 + lax.erf(inner * (1.0 / math.sqrt(2.0))))


def ff_fwd_kernel(hidden_ref, exp_ref, red_ref, par_ref, feed_ref):
    rows = hidden_ref.shape[0] // 2
    bent = row(par_ref, THRESHOLD)

    def block(b, carry):
        here = pl.ds(pl.multiple_of(b * rows, rows), rows)
        inner = nn(hidden_ref[here, :], exp_ref[...]) + bent
        feed_ref[here, :] = nn((inner * cumulative(inner)).astype(BF16), red_ref[...]).astype(BF16)
        return carry

    lax.fori_loop(0, 2, block, 0)


def ff_bwd_kernel(hidden_ref, rows_ref, sel_ref, exp_ref, red_ref, par_ref, back_ref, dexp_ref, dred_ref, thr_ref):
    groups = sel_ref.shape[0]
    few = jnp.concatenate([nn(sel_ref[q], hidden_ref[q]).astype(BF16) for q in range(groups)], 0)
    inner = nn(few, exp_ref[...]) + row(par_ref, THRESHOLD)
    weight = cumulative(inner)
    active = (inner * weight).astype(BF16)
    slope = weight + inner * jnp.exp(-0.5 * inner * inner) * (1.0 / math.sqrt(2.0 * math.pi))
    rows = rows_ref[...]
    d_inner = (nt(rows, red_ref[...]) * slope).astype(BF16)
    back_ref[...] = nt(d_inner, exp_ref[...]).astype(BF16)
    thr_ref[...] = jnp.sum(d_inner.astype(F32), 0, keepdims=True)
    dexp_ref[...] = tn(few, d_inner).astype(BF16)
    dred_ref[...] = tn(active, rows).astype(BF16)


def shards(tokens, cotangent, selected, buckets, projector, intercepts, combiner, offset, relative, stretch, uplift,
           expander, threshold, reducer, residue, amplify, displace):
    quarter, width = tokens.shape
    cols = projector.shape[2]
    part = projector.shape[1]
    n, group = lax.axis_size("dp"), lax.axis_size("tensor")
    classes = relative.shape[0]
    keep = -(-(quarter * 2 // 5) // 16) * 16
    S, V = jax.ShapeDtypeStruct, pltpu.VMEM
    packed = jnp.concatenate([projector[0], projector[1], projector[2], combiner], 1)
    picks = jnp.broadcast_to(selected.astype(F32)[None, :], (8, quarter))
    bias = intercepts.reshape(1, 3 * cols)
    span = buckets.shape[0] + 1
    bcol = jnp.concatenate([buckets[::-1], jnp.full((1,), -1, jnp.int32)]).reshape(span, 1)
    params = jnp.stack([v.astype(F32) for v in (offset, residue, stretch, uplift, amplify, displace, threshold, threshold)])

    x, w, chosen = comm_call(
        functools.partial(enter_kernel, n), 1,
        (S((group, quarter, width), BF16), S((n, part, width), BF16), S((group, 8, quarter), F32)),
        [], n + 8, (tokens, packed, picks), "enter")
    x2, w2 = x.reshape(group * quarter, width), w.reshape(n * part, width)
    probs, mixed, table, ctx, first, sel = attn_fwd(x2, w2, bias, relative, bcol, chosen, keep)
    hidden, mid, unit, inverse = comm_call(
        functools.partial(mid_kernel, n), 2,
        (S((group, quarter, width), BF16), S((quarter, width), F32), S((quarter, width), F32), S((quarter, 128), F32)),
        [V((3, quarter, width), BF16)], 8, (first.reshape(group, quarter, width), tokens, params), "mid")
    feed = pl.pallas_call(ff_fwd_kernel, out_shape=S((group * quarter, width), BF16), name="ff_fwd")(
        hidden.reshape(group * quarter, width), expander, reducer, params)
    result, d_end, d_rows, small = comm_call(
        functools.partial(end_kernel, n), 3,
        (S((quarter, width), BF16), S((quarter, width), F32), S((group, keep, width), BF16), S((8, width), F32)),
        [V((3, quarter, width), BF16)], 8, (feed.reshape(group, quarter, width), mid, cotangent, sel, params), "end")
    back, dexp, dred, thr = pl.pallas_call(
        ff_bwd_kernel,
        out_shape=(S((group * keep, width), BF16), S(expander.shape, BF16), S(reducer.shape, BF16), S((1, threshold.shape[0]), F32)),
        name="ff_bwd")(hidden, d_rows.reshape(group * keep, width), sel, expander, reducer, params)
    d_mid, d_attn, small = comm_call(
        functools.partial(back_kernel, n), 4,
        (S((quarter, width), F32), S((group, keep, width), BF16), S((8, width), F32)),
        [V((3, keep, width), BF16)], 8, (back.reshape(group, keep, width), d_end, unit, inverse, sel, params, small), "back")
    grads, input_part, rel_part, small = attn_bwd(x2, w2, relative, bcol, probs, mixed, table, ctx, d_attn.reshape(group * keep, width), sel, small, thr)
    ring = (n, width // n, width)
    totals = comm_call(
        functools.partial(total_kernel, n), 5,
        (S((n, expander.shape[0] // n, width), BF16), S((n, reducer.shape[0] // n, width), BF16)),
        [V((2, n // 2, expander.shape[0] // n, width), BF16), V((2, n // 2, reducer.shape[0] // n, width), BF16)],
        4 * n, (dexp.reshape(n, -1, width), dred.reshape(n, -1, width)), "totals")
    lines = classes // group // n
    weights, tokens_grad, relative_grad, sums = comm_call(
        functools.partial(exit_kernel, n), 6,
        (S((part, width), F32), S((quarter, width), F32), S((group, n, lines, width), BF16), S((8, width), F32)),
        [V((2, n // 2, part, width), BF16), V((3, quarter, width), BF16), V((3, classes // group, width), BF16), V((n, lines, width), BF16),
         V((2, n // 2, lines, width), BF16), V((n, 8, width), F32), V((3, 8, width), F32)],
        4 * n + 16, (grads.reshape(n, part, width), input_part.reshape(group, quarter, width), rel_part.reshape(group, classes // group, width), small, d_mid), "exit")
    projector_grad = jnp.stack([weights[:, :cols], weights[:, cols : 2 * cols], weights[:, 2 * cols : 3 * cols]])
    return (result, tokens_grad, projector_grad, sums[BIAS, : 3 * cols].reshape(3, cols), weights[:, 3 * cols :], sums[OFFSET],
            relative_grad.astype(F32).reshape(classes, width), sums[STRETCH], sums[UPLIFT], totals[0].astype(F32).reshape(expander.shape),
            sums[THRESHOLD], totals[1].astype(F32).reshape(reducer.shape), sums[RESIDUE], sums[AMPLIFY], sums[DISPLACE])


def solution(mesh):
    both = P(("dp", "tensor"), None)
    return jax.shard_map(
        shards,
        mesh=mesh,
        in_specs=(both, both, P(("dp", "tensor")), P(), P(None, "dp", "tensor"), P(None, "tensor"), P("dp", "tensor"), P(), P(), P(), P(),
                  P(None, "tensor"), P("tensor"), P("tensor", None), P(), P(), P()),
        out_specs=(both, both, P(None, "dp", "tensor"), P(None, "tensor"), P("dp", "tensor"), P(), P(), P(), P(),
                   P(None, "tensor"), P("tensor"), P("tensor", None), P(), P(), P()),
        check_vma=False,
    )
```

time: 543 us -> 244 us (0.45)
  waiting for transfers between devices: 350 us -> 0 us
  Pallas kernels: 35.7 us -> 217 us
  blocking collectives: 96 us -> 0 us
  matrix products: 14.6 us -> 0 us
  other arithmetic: 23 us -> 8.57 us
  between operations: 14.6 us -> 0.74 us
  local copies, waits for them, and re-layouts: 8.64 us -> 16.6 us
    pallas_call x0 -> x8, Pallas kernels: none -> 181 us  [the longest x6 171 us: comm_call(): pl.pallas_call(kernel, out_shape=outs, scratch_shapes=list(scratch) + [pl...]
    psum x2 -> x0, waiting for transfers between devices: 174 us -> none  [the longest x1 109 us: shards(): expander_grad, reducer_grad = lax.psum((expander_part, reducer_part), 'dp')]
    reduce_scatter x5 -> x0, waiting for transfers between devices: 144 us -> none  [the longest x1 66.4 us: shards(): lax.psum_scatter(grads, 'dp', scatter_dimension=0, tiled=True).astype(F32)]
    psum x2 -> x0, blocking collectives: 59.5 us -> none  [the longest x1 37.1 us: shards(): small = lax.psum(small, ('dp', 'tensor'))]
    all_gather x5 -> x0, blocking collectives: 36.5 us -> none  [the longest x1 10.5 us: shards(): x = lax.all_gather(tokens, 'tensor', axis=0, tiled=True)]
    all_gather x1 -> x0, waiting for transfers between devices: 30.9 us -> none  [shards(): w = lax.all_gather(packed, 'dp', axis=0, tiled=True)]
    dot_general x10 -> x0, matrix products: 14.6 us -> none  [the longest x3 6.02 us: tn(): lax.dot_general(a, b, (((0,), (0,)), ((), ())), preferred_element_type=F32)]
    convert_element_type x10 -> x1, other arithmetic: 10.4 us -> 0.66 us  [shards(): picks = jnp.broadcast_to(selected.astype(F32)[None, :], (8, quarter))]
  transfers between devices with their start and end apart: 8 -> 0, of which waited for: 8 -> 0; matrix products, arithmetic and copies ran while one was open for 4% -> 0% of each run, Pallas kernels for 0% -> 0%
where the time goes in v2:
time: 244 us; the launch traced here: 243 us
  Pallas kernels  217 us (89%)
  local copies, waits for them, and re-layouts  16.6 us (7%)
  other arithmetic  8.57 us (4%)
    pallas_call x6, Pallas kernels, comm_call(): pl.pallas_call(kernel, out_shape=outs, scratch_shapes=list(scratch) + [pl...  171 us
    pallas_call x1, Pallas kernels, attn_bwd(): pl.pallas_call(functools.partial(attn_bwd_kernel, scale), out_shape=(S((w...  21.4 us
    pallas_call x1, Pallas kernels, attn_fwd(): pl.pallas_call(functools.partial(attn_fwd_kernel, scale), out_shape=(S((h...  14.7 us
    another operation x8, local copies, waits for them, and re-layouts, shards(): jnp.stack([v.astype(F32) for v in (offset, residue, stretch, uplift, ampl...  5.45 us
    pallas_call x1, Pallas kernels, shards(): pl.pallas_call(ff_bwd_kernel, out_shape=(S((group * keep, width), BF16),...  5.13 us

profile of v2, /device:TPU:0, one launch (start us, length us, event | category | flops | bytes accessed | tf_op | source)
XLA Modules:
  0.0 242.8 jit_solution(1125053278535266710)
XLA Ops:
  0.6 0.7 convert_element_type.2
  1.3 1.3 reshape.96.bias_ref
  2.6 0.7 reshape.115
  3.3 0.7 stack.50
  4.0 0.7 stack.51
  4.7 0.7 reshape.117
  5.4 0.7 reshape.116
  6.1 0.7 stack.52
  6.8 0.7 stack.53
  8.7 0.8 reverse
  9.6 0.9 slice_bitcast_fusion.5
  10.5 1.6 pad_maximum_fusion.1.own_ref
  12.0 1.1 copy.32.bcol_ref
  13.1 25.1 %enter.1 = (bf16[4,128,768]{2,1,0:T(8,128)(2,1)}, bf16[8,96,768]{2,1,0:T(8,128)(2,1)}, f32[4,8,128]{2,1,0:T(8,128)}) custom-call(bf16[128,768]{1,0:T(8,128)(2,1)} %tok_ref.3, bf16[96,768]{1,0:T(8,128)(2,1)} %pad_maximum_fusion.1.own_ref, f32[8,128]{1,0:T(8,128)} %broadcast_in_dim.2.pick_ref), custom_call_target="tpu_custom_call" | custom-call | tf_op jit(solution)/shard_map/enter/pallas_call | solution.py:336
  38.2 14.7 %attn_fwd.1 = (f32[3,512,512]{2,1,0:T(8,128)}, bf16[512,576]{1,0:T(8,128)(2,1)}, bf16[1024,384]{1,0:T(8,128)(2,1)}, bf16[512,192]{1,0:T(8,128)(2,1)}, bf16[512,7...) custom-call(bf16[512,768]{1,0:T(8,128)(2,1)} %bitcast.38, bf16[768,768]{1,0:T(8,128)(2,1)} %bitcast.36, ...), custom_call_target="tpu_custom_call" | custom-call | tf_op jit(solution)/shard_map/attn_fwd/pallas_call | solution.py:83
  52.9 18.1 %mid.1 = (bf16[4,128,768]{2,1,0:T(8,128)(2,1)}, f32[128,768]{1,0:T(8,128)}, f32[128,768]{1,0:T(8,128)}, f32[128,128]{1,0:T(8,128)}) custom-call(bf16[4,128,768]{2,1,0:T(8,128)(2,1)} %bitcast.47, bf16[128,768]{1,0:T(8,128)(2,1)} %tok_ref.3, f32[8,768]{1,0:T(8,128)} %stack.56.par_ref), custom_call_target="tpu_custom_call" | custom-call | tf_op jit(solution)/shard_map/mid/pallas_call | solution.py:336
  71.0 4.6 %ff_fwd.1 = bf16[512,768]{1,0:T(8,128)(2,1)} custom-call(bf16[512,768]{1,0:T(8,128)(2,1)} %bitcast.40, bf16[768,768]{1,0:T(8,128)(2,1)} %exp_ref.3, bf16[768,768]{1,0:T(8,128)(2,1)} %red_ref.3, f32[8,768]{1,0:T(8,128)} %stack.56.par_ref), custom_call_target="tpu_custom_call" | custom-call | tf_op jit(solution)/shard_map/ff_fwd/pallas_call | solution.py:551
  75.6 16.0 %end.1 = (bf16[128,768]{1,0:T(8,128)(2,1)}, f32[128,768]{1,0:T(8,128)}, bf16[4,64,768]{2,1,0:T(8,128)(2,1)}, f32[8,768]{1,0:T(8,128)}) custom-call(bf16[4,128,768]{2,1,0:T(8,128)(2,1)} %bitcast.41, f32[128,768]{1,0:T(8,128)} %get-tuple-element.54.mid_ref, bf16[128,768]{1,0:T(8,128)(2,1)} %cot_ref.1, bf16[4,64,128]{2,1,0:T(8,128)(2,1)} %get-tuple-element.55.sel_ref, ...), custom_call_target="tpu_custom_call" | custom-call | tf_op jit(solution)/shard_map/end/pallas_call | solution.py:336
  91.6 5.1 %ff_bwd.1 = (bf16[256,768]{1,0:T(8,128)(2,1)}, bf16[768,768]{1,0:T(8,128)(2,1)}, bf16[768,768]{1,0:T(8,128)(2,1)}, f32[1,768]{1,0:T(1,128)}) custom-call(bf16[4,128,768]{2,1,0:T(8,128)(2,1)} %get-tuple-element.53.hidden_ref, bf16[256,768]{1,0:T(8,128)(2,1)} %bitcast.49, bf16[4,64,128]{2,1,0:T(8,128)(2,1)} %get-tuple-element.55.sel_ref, ...), custom_call_target="tpu_custom_call" | custom-call | tf_op jit(solution)/shard_map/ff_bwd/pallas_call | solution.py:557
  96.7 14.5 %back.1 = (f32[128,768]{1,0:T(8,128)}, bf16[4,64,768]{2,1,0:T(8,128)(2,1)}, f32[8,768]{1,0:T(8,128)}) custom-call(bf16[4,64,768]{2,1,0:T(8,128)(2,1)} %bitcast.50, f32[128,768]{1,0:T(8,128)} %get-tuple-element.63.dend_ref, f32[128,768]{1,0:T(8,128)} %get-tuple-element.64.unit_ref, f32[128,128]{1,0:T(8,128)} %get-tuple-element.65.inverse_ref, ...), custom_call_target="tpu_custom_call" | custom-call | tf_op jit(solution)/shard_map/back/pallas_call | solution.py:336
  111.2 21.4 %attn_bwd.1 = (bf16[768,768]{1,0:T(8,128)(2,1)}, bf16[512,768]{1,0:T(8,128)(2,1)}, bf16[512,768]{1,0:T(8,128)(2,1)}, f32[8,768]{1,0:T(8,128)}) custom-call(bf16[512,768]{1,0:T(8,128)(2,1)} %bitcast.39, bf16[768,768]{1,0:T(8,128)(2,1)} %bitcast.37, bf16[512,768]{1,0:T(8,128)(2,1)} %rel_ref.3, s32[1024,1]{1,0:T(8,128)} %copy.32.bcol_ref, ...), custom_call_target="tpu_custom_call" | custom-call | tf_op jit(solution)/shard_map/attn_bwd/pallas_call | solution.py:179
  132.6 45.2 %exit.1 = (f32[96,768]{1,0:T(8,128)}, f32[128,768]{1,0:T(8,128)}, bf16[4,8,16,768]{3,2,1,0:T(8,128)(2,1)}, f32[8,768]{1,0:T(8,128)}) custom-call(bf16[8,96,768]{2,1,0:T(8,128)(2,1)} %bitcast.42, bf16[4,128,768]{2,1,0:T(8,128)(2,1)} %bitcast.45, bf16[4,128,768]{2,1,0:T(8,128)(2,1)} %bitcast.46, f32[8,768]{1,0:T(8,128)} %get-tuple-element.73.small_ref, ...), custom_call_target="tpu_custom_call" | custom-call | tf_op jit(solution)/shard_map/exit/pallas_call | solution.py:336
  177.8 0.8 slice_reduce_fusion.7
  178.7 0.7 reshape_squeeze.3
  179.3 1.7 slice_reduce_fusion
  181.1 1.8 fusion
  182.9 0.7 pad_maximum_fusion
  183.6 1.3 bitcast_convert_fusion.2
  184.9 52.2 %totals.1 = (bf16[8,96,768]{2,1,0:T(8,128)(2,1)}, bf16[8,96,768]{2,1,0:T(8,128)(2,1)}) custom-call(bf16[8,96,768]{2,1,0:T(8,128)(2,1)} %bitcast.43, bf16[8,96,768]{2,1,0:T(8,128)(2,1)} %bitcast.44), custom_call_target="tpu_custom_call" | custom-call | tf_op jit(solution)/shard_map/totals/pallas_call | solution.py:336
  237.1 4.2 %bitcast_convert_fusion = (f32[768,768]{1,0:T(8,128)}, f32[768,768]{1,0:T(8,128)}) fusion(bf16[8,96,768]{2,1,0:T(8,128)(2,1)} %get-tuple-element.82, bf16[8,96,768]{2,1,0:T(8,128)(2,1)} %get-tuple-element.81), kind=kLoop, calls=%fused_computation | loop fusion | flops 1179648 | bytes 7077888 | tf_op jit(solution)/shard_map/reshape | solution.py:582
  241.3 0.7 copy.36
  242.0 0.7 copy.37
  (10 shorter events, 1.4 us)
Async XLA Ops:
  177.8 5.8 %copy-start = (bf16[4,8,16,768]{3,2,1,0:T(8,128)(2,1)S(1)}, bf16[4,8,16,768]{3,2,1,0:T(8,128)(2,1)}, u32[]{:S(2)}) copy-start(bf16[4,8,16,768]{3,2,1,0:T(8,128)(2,1)} %get-tuple-element.78) | copy-start | bytes 2359300
  237.1 4.3 %copy-start.2 = (bf16[128,768]{1,0:T(8,128)(2,1)S(1)}, bf16[128,768]{1,0:T(8,128)(2,1)}, u32[]{:S(2)}) copy-start(bf16[128,768]{1,0:T(8,128)(2,1)} %get-tuple-element.114) | copy-start | bytes 589828
  237.1 4.9 %copy-start.1 = (f32[128,768]{1,0:T(8,128)S(1)}, f32[128,768]{1,0:T(8,128)}, u32[]{:S(2)}) copy-start(f32[128,768]{1,0:T(8,128)} %get-tuple-element.115) | copy-start | bytes 1179652

commit v3 on v1

v3 whole, which is shorter than its diff:
```python
import functools
import math
from types import SimpleNamespace

import jax
import jax.numpy as jnp
from jax import lax
from jax.experimental import pallas as pl
from jax.experimental.pallas import tpu as pltpu
from jax.sharding import PartitionSpec as P

HEAD_DIM = 64
BLK = 128
EPSILON = 1e-05
F32, BF16 = jnp.float32, jnp.bfloat16
MESH = pl.DeviceIdType.MESH
OFFSET, RESIDUE, STRETCH, UPLIFT, AMPLIFY, DISPLACE, THRESHOLD, BIAS = range(8)


def nn(a, b):
    return lax.dot_general(a, b, (((1,), (0,)), ((), ())), preferred_element_type=F32)


def nt(a, b):
    return lax.dot_general(a, b, (((1,), (1,)), ((), ())), preferred_element_type=F32)


def tn(a, b):
    return lax.dot_general(a, b, (((0,), (0,)), ((), ())), preferred_element_type=F32)


def flat(value):
    return value.reshape(value.shape[0] * value.shape[1], value.shape[2])


def line(ref):
    return ref[...].astype(F32).reshape(1, -1)


def exchange():
    return (lax.broadcasted_iota(jnp.int32, (BLK, BLK), 0) + lax.broadcasted_iota(jnp.int32, (BLK, BLK), 1) == BLK - 1).astype(BF16)


def at_place(spot, n):
    return jnp.where(spot < n // 2, 2 * spot, 2 * (n - 1 - spot) + 1)


def place_of(index, n):
    return jnp.where(index % 2 == 0, index // 2, n - 1 - index // 2)


class Links:
    def __init__(self, n, send, recv):
        self.n, self.send, self.recv, self.used = n, send, recv, 0
        self.dp = lax.axis_index("dp")
        self.me = lax.axis_index("tensor")
        self.spot = place_of(self.dp, n)
        self.right = (at_place((self.spot + 1) % n, n), self.me)
        self.left = (at_place((self.spot + n - 1) % n, n), self.me)
        core = self.me % 2
        self.mate = self.me + 1 - 2 * core
        self.other = (self.me + 2) % 4
        self.twin = (self.dp, self.mate)
        self.across = (self.dp, self.other)

    def chunk(self, shift):
        return at_place((self.spot + shift + 2 * self.n) % self.n, self.n)

    def greet(self):
        barrier = pltpu.get_barrier_semaphore()
        for peer in (self.left, self.right, self.twin, self.across):
            pl.semaphore_signal(barrier, inc=1, device_id=peer, device_id_type=MESH)
        pl.semaphore_wait(barrier, 4)

    def start(self, src, dst, peer):
        k = self.used
        self.used += 1
        copy = pltpu.make_async_remote_copy(src_ref=src, dst_ref=dst, send_sem=self.send.at[k], recv_sem=self.recv.at[k],
                                            device_id=peer, device_id_type=MESH)
        copy.start()
        return copy


def step(*tasks):
    for task in tasks:
        next(task, None)


def finish(*tasks):
    tasks = list(tasks)
    while tasks:
        for task in list(tasks):
            try:
                next(task)
            except StopIteration:
                tasks.remove(task)


def ring_gather(links, full, low, high, cut, own=None):
    n = links.n
    half = n // 2
    sides = ((links.right, -1, slice(low, cut)), (links.left, 1, slice(cut, high)))
    made = []
    for s in range(half):
        for k, (peer, way, part) in enumerate(sides):
            if s:
                made[2 * (s - 1) + k].wait_recv()
            index = links.chunk(way * s)
            if s < half - 1:
                part = slice(low, high)
            dst = full.at[index, :, part]
            made.append(links.start(dst if s or own is None else own.at[:, part], dst, peer))
        yield
    for k in range(2):
        made[2 * (half - 1) + k].wait_recv()
    for copy in made:
        copy.wait_send()


def ring_scatter(links, parts, slots, done, low, high, cut):
    n = links.n
    half = n // 2
    sides = ((links.right, 1, slice(low, cut), slice(cut, high)), (links.left, -1, slice(cut, high), slice(low, cut)))
    here = slice(low, high)
    made = []
    for s in range(half):
        for k, (peer, way, part, rest) in enumerate(sides):
            index = links.chunk(way * (half - s))
            if s == 0:
                src, dst = parts.at[index, :, part], slots.at[k, 0, :, part]
            else:
                made[2 * (s - 1) + k].wait_recv()
                held = slots.at[k, s - 1]
                if s == 1:
                    held[:, part] = (held[:, part].astype(F32) + parts[index, :, part].astype(F32)).astype(BF16)
                    held[:, rest] = parts[index, :, rest]
                else:
                    held[:, here] = (held[:, here].astype(F32) + parts[index, :, here].astype(F32)).astype(BF16)
                src, dst = held.at[:, here], slots.at[k, s, :, here]
            made.append(links.start(src, dst, peer))
        yield
    for k in range(2):
        made[2 * (half - 1) + k].wait_recv()
    done(parts[links.dp, :, here].astype(F32) + slots[0, half - 1, :, here].astype(F32) + slots[1, half - 1, :, here].astype(F32))
    for copy in made:
        copy.wait_send()


def group_gather(links, full, own=None):
    mine = full.at[links.me]
    src = mine if own is None else own
    over = links.start(src, mine, links.across)
    near = links.start(src, mine, links.twin)
    yield
    over.wait_recv()
    block = full.at[links.other]
    on = links.start(block, block, links.twin)
    yield
    near.wait_recv()
    on.wait_recv()
    for copy in (over, near, on):
        copy.wait_send()


def group_scatter(links, parts, slots, done):
    first = links.start(parts.at[(links.mate + 2) % 4], slots.at[0], links.twin)
    second = links.start(parts.at[links.mate], slots.at[1], links.twin)
    yield
    first.wait_recv()
    slots[0] = (slots[0].astype(F32) + parts[links.other].astype(F32)).astype(BF16)
    over = links.start(slots.at[0], slots.at[2], links.across)
    yield
    second.wait_recv()
    over.wait_recv()
    done(parts[links.me].astype(F32) + slots[1].astype(F32) + slots[2].astype(F32))
    for copy in (first, second, over):
        copy.wait_send()


def normalize(value, gain, shift):
    mean = jnp.mean(value, -1, keepdims=True)
    center = value - mean
    inverse = lax.rsqrt(jnp.mean(center * center, -1, keepdims=True) + EPSILON)
    unit = center * inverse
    return (unit * gain + shift, unit, inverse)


def normalize_back(incoming, gain, unit, inverse):
    scaled = incoming * gain
    result = inverse * (scaled - jnp.mean(scaled, -1, keepdims=True) - unit * jnp.mean(scaled * unit, -1, keepdims=True))
    return (result, jnp.sum(incoming * unit, 0, keepdims=True), jnp.sum(incoming, 0, keepdims=True))


def cumulative(inner):
    return 0.5 * (1.0 + lax.erf(inner * (1.0 / math.sqrt(2.0))))


def enter(links, c):
    cols = c.combiner.shape[1]
    for m in range(3):
        c.own[:, cols * m : cols * (m + 1)] = c.projector[m]
    c.own[:, 3 * cols :] = c.combiner[...]
    c.pick[...] = jnp.broadcast_to(c.selected[...].astype(F32).reshape(1, -1), c.pick.shape)
    links.greet()
    c.x[links.me] = c.tokens[...]
    c.w[links.dp] = c.own[...]
    c.chosen[links.me] = c.pick[...]
    width = c.own.shape[1]
    finish(group_gather(links, c.x, c.tokens), ring_gather(links, c.w, 0, width // 2, width // 2 - BLK, c.own),
           ring_gather(links, c.w, width // 2, width, width // 2 + BLK, c.own), group_gather(links, c.chosen, c.pick))


def attend(links, c, scale):
    length = c.mixed.shape[0]
    cols = c.combiner.shape[1]
    classes = c.relative.shape[0]
    blocks = length // BLK
    win = length + BLK
    flip = exchange()
    bias = jnp.concatenate([c.intercepts[m : m + 1, :].astype(F32) for m in range(3)], 1)
    weights = flat(c.w[...])
    c.mixed[...] = (nn(flat(c.x[...]), weights[:, : 3 * cols]) + bias).astype(BF16)
    pos = (nn(c.relative[...], weights[:, : 2 * cols]) + bias[:, : 2 * cols]).astype(BF16)
    turned = c.buckets[...].astype(F32).T
    groups = c.buckets.shape[0]
    kinds = lax.broadcasted_iota(jnp.int32, (BLK, classes), 1).astype(F32)
    for g in range(groups):
        rows = slice(BLK * (groups - 1 - g), BLK * (groups - g))
        c.spread[rows, :] = nn(flip, (turned[:, g : g + 1] == kinds).astype(BF16)).astype(BF16)
        c.table[rows, :] = nn(c.spread[rows, :], pos).astype(BF16)
    quarter = c.chosen.shape[2]
    below = (lax.broadcasted_iota(jnp.int32, (quarter, quarter), 0) <= lax.broadcasted_iota(jnp.int32, (quarter, quarter), 1)).astype(BF16)
    order = lax.broadcasted_iota(jnp.int32, c.sel.shape[1:], 0).astype(F32) + 1.0
    for q in range(c.sel.shape[0]):
        rank = nn(c.chosen[q].astype(BF16), below)[:1]
        c.sel[q] = jnp.where(rank == order, c.chosen[q, :1], 0.0).astype(BF16)
    lanes = lax.broadcasted_iota(jnp.int32, (1, cols), 1) // HEAD_DIM
    c.acc[...] = jnp.zeros_like(c.acc)

    def head(h):
        own = lanes == h
        pick = lambda v: jnp.where(own, v, jnp.zeros_like(v))
        key_h = pick(c.mixed[:, cols : 2 * cols])
        for b in range(blocks):
            start = length - BLK * (b + 1)
            rows = slice(BLK * b, BLK * (b + 1))
            wide = nt(key_h[rows], c.table[start : start + win, :cols])
            c.far[:, rows] = pltpu.roll(wide, win - BLK + 1, 1, stride=1, stride_axis=0)[:, :length].T
        value_h = pick(c.mixed[:, 2 * cols : 3 * cols])
        for b in range(blocks):
            start = length - BLK * (b + 1)
            rows = slice(BLK * b, BLK * (b + 1))
            query = pick(c.mixed[rows, :cols])
            wide = nt(query, c.table[start : start + win, cols : 2 * cols])
            near = pltpu.roll(wide, win - BLK + 1, 1, stride=1, stride_axis=0)[:, :length]
            scores = (nt(query, key_h) + near + c.far[rows, :]) * scale
            top = jnp.max(scores, -1, keepdims=True)
            weights = jnp.exp(scores - top)
            probs = weights / jnp.sum(weights, -1, keepdims=True)
            c.probs[h, rows, :] = probs
            c.acc[rows, :] += nn(probs.astype(BF16), value_h)

    for h in range(cols // HEAD_DIM):
        head(h)
    c.ctx[...] = c.acc[...].astype(BF16)
    c.part[...] = nt(c.ctx[...], weights[:, 3 * cols :]).astype(BF16).reshape(c.part.shape)


def middle(links, c):
    def done(total):
        mid, unit, inverse = normalize(c.tokens[...].astype(F32) + total + line(c.offset), line(c.stretch), line(c.uplift))
        c.mid[...] = mid
        c.unit[...] = unit
        c.inverse[...] = jnp.broadcast_to(inverse, c.inverse.shape)
        c.hidden[links.me] = mid.astype(BF16)

    finish(group_scatter(links, c.part, c.part_slots, done))
    finish(group_gather(links, c.hidden))


def feed(links, c):
    bent = line(c.threshold)
    for b in range(2):
        inner = nn(flat(c.hidden[2 * b : 2 * b + 2]), c.expander[...]) + bent
        value = nn((inner * cumulative(inner)).astype(BF16), c.reducer[...]).astype(BF16)
        c.feed[2 * b : 2 * b + 2] = value.reshape((2,) + c.feed.shape[1:])


def end(links, c):
    mine = c.sel[links.me]
    marks = tn(mine, jnp.ones((mine.shape[0], BLK), BF16))[:, :1]

    def done(total):
        value, unit, inverse = normalize(c.mid[...] + total + line(c.residue), line(c.amplify), line(c.displace))
        c.result[...] = value.astype(BF16)
        d_end, gain, shift = normalize_back(c.cotangent[...].astype(F32) * marks, line(c.amplify), unit, inverse)
        c.d_end[...] = d_end
        low = d_end.astype(BF16)
        c.d_rows[links.me] = nn(mine, low).astype(BF16)
        c.small[AMPLIFY : AMPLIFY + 1, :] = gain
        c.small[DISPLACE : DISPLACE + 1, :] = shift
        c.small[RESIDUE : RESIDUE + 1, :] = jnp.sum(low.astype(F32), 0, keepdims=True)

    finish(group_scatter(links, c.feed, c.feed_slots, done))
    finish(group_gather(links, c.d_rows))


def feed_back(links, c):
    few = jnp.concatenate([nn(c.sel[q], c.hidden[q]).astype(BF16) for q in range(c.sel.shape[0])], 0)
    inner = nn(few, c.expander[...]) + line(c.threshold)
    weight = cumulative(inner)
    active = (inner * weight).astype(BF16)
    slope = weight + inner * jnp.exp(-0.5 * inner * inner) * (1.0 / math.sqrt(2.0 * math.pi))
    rows = flat(c.d_rows[...])
    d_inner = (nt(rows, c.reducer[...]) * slope).astype(BF16)
    c.back[...] = nt(d_inner, c.expander[...]).astype(BF16).reshape(c.back.shape)
    c.small[THRESHOLD : THRESHOLD + 1, :] = jnp.sum(d_inner.astype(F32), 0, keepdims=True)
    c.d_exp[...] = tn(few, d_inner).astype(BF16).reshape(c.d_exp.shape)
    c.d_red[...] = tn(active, rows).astype(BF16).reshape(c.d_red.shape)


def total(links, parts, slots, full, cut):
    def done(value):
        full[links.dp] = value.astype(BF16)

    width = parts.shape[2]
    yield from ring_scatter(links, parts, slots, done, 0, width, cut)
    yield from ring_gather(links, full, 0, width, cut)


def middle_back(links, c, beside):
    mine = c.sel[links.me]

    def done(total):
        high = total.astype(BF16)
        spread = tn(mine, high) + tn(mine, (total - high.astype(F32)).astype(BF16))
        d_mid, gain, shift = normalize_back(c.d_end[...] + spread, line(c.stretch), c.unit[...], c.inverse[:, :1])
        c.d_mid[...] = d_mid
        low = d_mid.astype(BF16)
        c.d_attn[links.me] = nn(mine, low).astype(BF16)
        c.small[STRETCH : STRETCH + 1, :] = gain
        c.small[UPLIFT : UPLIFT + 1, :] = shift
        c.small[OFFSET : OFFSET + 1, :] = jnp.sum(low.astype(F32), 0, keepdims=True)

    task = group_scatter(links, c.back, c.back_slots, done)
    step(task)
    step(*beside)
    finish(task)
    task = group_gather(links, c.d_attn)
    step(task)
    step(*beside)
    finish(task)


def attend_back(links, c, scale, beside, leave):
    length = c.mixed.shape[0]
    cols = c.combiner.shape[1]
    span = c.table.shape[0]
    blocks = length // BLK
    win = length + BLK
    flip = exchange()
    weights = flat(c.w[...])
    d_attn = flat(c.d_attn[...])
    little = nn(d_attn, weights[:, 3 * cols :]).astype(BF16)
    keep = c.sel.shape[1]
    ctx_few = []
    for b in range(blocks):
        rows = slice(BLK * b, BLK * (b + 1))
        c.dctx[rows, :] = tn(c.sel[b], little[keep * b : keep * (b + 1)]).astype(BF16)
        ctx_few.append(nn(c.sel[b], c.ctx[rows, :]).astype(BF16))
        c.turn_t[:cols, rows] = tn(c.mixed[rows, :cols], flip).astype(BF16)
        c.turn_t[cols:, rows] = tn(c.mixed[rows, cols : 2 * cols], flip).astype(BF16)
    c.dctx_t[...] = c.dctx[...].T
    lanes = lax.broadcasted_iota(jnp.int32, (1, cols), 1) // HEAD_DIM
    c.dq[...] = jnp.zeros_like(c.dq)
    c.dk[...] = jnp.zeros_like(c.dk)
    c.dpos_t[...] = jnp.zeros_like(c.dpos_t)
    blank = jnp.zeros((BLK, BLK), F32)

    def head(h):
        own = lanes == h
        pick = lambda v: jnp.where(own, v, jnp.zeros_like(v))
        mine = slice(h * HEAD_DIM, (h + 1) * HEAD_DIM)
        low = slice(cols + h * HEAD_DIM, cols + (h + 1) * HEAD_DIM)
        key_h = pick(c.mixed[:, cols : 2 * cols])
        query_h = pick(c.mixed[:, :cols])
        value = c.mixed[:, 2 * cols : 3 * cols]
        posq_h = pick(c.table[:, :cols])
        posk_h = pick(c.table[:, cols : 2 * cols])
        so_far = jnp.zeros((HEAD_DIM, length), F32)
        for b in range(blocks):
            start = length - BLK * (b + 1)
            rows = slice(BLK * b, BLK * (b + 1))
            probs = c.probs[h, rows, :]
            dprobs = nt(pick(c.dctx[rows, :]), value)
            dscores = (probs * (dprobs - jnp.sum(probs * dprobs, -1, keepdims=True))).astype(BF16)
            c.ds[rows, :] = dscores
            so_far += nn(c.dctx_t[mine, rows], probs.astype(BF16))
            turned = nn(flip, dscores)
            moved = pltpu.roll(jnp.concatenate([turned, blank], 1), 0, 1, stride=1, stride_axis=0).astype(BF16)
            c.dq[rows, :] += nn(turned.astype(BF16), key_h) + nn(moved, posk_h[start : start + win])
            c.dpos_t[low, start : start + win] += nn(c.turn_t[mine, rows], moved)
        c.dv_t[mine, :] = so_far
        for b in range(blocks):
            start = length - BLK * (b + 1)
            rows = slice(BLK * b, BLK * (b + 1))
            turned = nt(flip, c.ds[:, rows])
            moved = pltpu.roll(jnp.concatenate([turned, blank], 1), 0, 1, stride=1, stride_axis=0).astype(BF16)
            c.dk[rows, :] += nn(turned.astype(BF16), query_h) + nn(moved, posq_h[start : start + win])
            c.dpos_t[mine, start : start + win] += nn(c.turn_t[low, rows], moved)

    for h in range(cols // HEAD_DIM):
        step(*beside)
        head(h)
    wide = c.dpos_t[...] * scale
    high = wide.astype(BF16)
    dpos = (nn(high, c.spread[...]) + nn((wide - high.astype(F32)).astype(BF16), c.spread[...])).T
    dpos_low = dpos.astype(BF16)
    c.rel_part[...] = nt(dpos_low, weights[:, : 2 * cols]).astype(BF16).reshape(c.rel_part.shape)
    leave("relative")
    order = lambda ref: jnp.concatenate([nn(flip, (ref[BLK * b : BLK * (b + 1), :] * scale).astype(BF16)).astype(BF16) for b in range(blocks)], 0)
    dmixed = jnp.concatenate([order(c.dq), order(c.dk), c.dv_t[...].T.astype(BF16)], 1)
    both = tn(flat(c.x[...]), dmixed)
    grads = jnp.concatenate([both[:, : 2 * cols] + tn(c.relative[...], dpos_low), both[:, 2 * cols :], tn(d_attn, jnp.concatenate(ctx_few, 0))], 1)
    c.grads[...] = grads.astype(BF16).reshape(c.grads.shape)
    leave("grads")
    c.in_part[...] = nt(dmixed, weights[:, : 3 * cols]).astype(BF16).reshape(c.in_part.shape)
    leave("tokens")
    sums = jnp.sum(dmixed.astype(F32), 0, keepdims=True)
    c.small[BIAS : BIAS + 1, : 2 * cols] = sums[:, : 2 * cols] + jnp.sum(dpos, 0, keepdims=True)
    c.small[BIAS : BIAS + 1, 2 * cols : 3 * cols] = sums[:, 2 * cols :]
    c.small[BIAS : BIAS + 1, 3 * cols :] = jnp.zeros((1, cols), F32)
    leave("small")


def leave_small(links, c):
    shared = lax.broadcasted_iota(jnp.int32, c.small.shape, 0) < THRESHOLD
    a = links.start(c.small, c.small_slots.at[0], links.twin)
    yield
    a.wait_recv()
    c.small_slots[1] = c.small[...] + jnp.where(shared, c.small_slots[0], 0.0)
    b = links.start(c.small_slots.at[1], c.small_slots.at[2], links.across)
    yield
    b.wait_recv()
    c.small_all[links.dp] = c.small_slots[1] + jnp.where(shared, c.small_slots[2], 0.0)
    yield from ring_gather(links, c.small_all, 0, c.small.shape[1], c.small.shape[1] // 2)
    a.wait_send()
    b.wait_send()
    c.sums[...] = jnp.sum(c.small_all[...], 0)


def leave_relative(links, c):
    def rel_done(total):
        c.rel_own[...] = total.astype(BF16).reshape(c.rel_own.shape)

    yield from group_scatter(links, c.rel_part, c.rel_slots, rel_done)
    mine = c.rel_all.at[links.me]

    def own_done(total):
        mine[links.dp] = total.astype(BF16)

    width = c.rel_own.shape[2]
    yield from ring_scatter(links, c.rel_own, c.rel_ring, own_done, 0, width, width // 2)
    yield from ring_gather(links, mine, 0, width, width // 2)
    yield from group_gather(links, c.rel_all)


def layer_kernel(n, names, *refs):
    c = SimpleNamespace(**dict(zip(names, refs)))
    links = Links(n, c.send, c.recv)
    scale = 1.0 / math.sqrt(3 * HEAD_DIM)
    width = c.tokens.shape[1]
    enter(links, c)
    attend(links, c, scale)
    middle(links, c)
    feed(links, c)
    end(links, c)
    feed_back(links, c)
    rings = (total(links, c.d_exp, c.exp_slots, c.exp_all, width // 2), total(links, c.d_red, c.red_slots, c.red_all, width // 2))
    step(*rings)
    middle_back(links, c, rings)

    def weights_done(low):
        def done(total):
            c.weights[:, low : low + width // 2] = total
        return done

    def tokens_done(total):
        c.d_tokens[...] = c.d_mid[...] + total

    tasks = {
        "relative": [leave_relative(links, c)],
        "grads": [ring_scatter(links, c.grads, c.grad_slots, weights_done(0), 0, width // 2, width // 2 - BLK),
                  ring_scatter(links, c.grads, c.grad_slots, weights_done(width // 2), width // 2, width, width // 2 + BLK)],
        "tokens": [group_scatter(links, c.in_part, c.in_slots, tokens_done)],
        "small": [leave_small(links, c)],
    }

    def leave(key):
        step(*tasks[key])
        if key == "grads":
            step(*tasks["relative"])

    attend_back(links, c, scale, rings, leave)
    step(*tasks["tokens"])
    finish(*tasks["relative"], *tasks["small"], *rings, *tasks["grads"], *tasks["tokens"])


def last_kernel(names, *refs):
    c = SimpleNamespace(**dict(zip(names, refs)))
    cols = c.combiner_grad.shape[1]
    c.out[...] = c.result[...]
    c.tokens_grad[...] = c.d_tokens[...]
    for m in range(3):
        c.projector_grad[m] = c.weights[:, cols * m : cols * (m + 1)]
        c.intercepts_grad[m : m + 1, :] = c.sums[BIAS : BIAS + 1, cols * m : cols * (m + 1)]
    c.combiner_grad[...] = c.weights[:, 3 * cols :]
    c.relative_grad[...] = c.rel_all[...].astype(F32)
    c.expander_grad[...] = c.exp_all[...].astype(F32)
    c.reducer_grad[...] = c.red_all[...].astype(F32)
    for key, k in (("offset", OFFSET), ("residue", RESIDUE), ("stretch", STRETCH), ("uplift", UPLIFT), ("amplify", AMPLIFY), ("displace", DISPLACE),
                   ("threshold", THRESHOLD)):
        ref = getattr(c, key + "_grad")
        ref[...] = c.sums[k : k + 1, :].reshape(ref.shape)


def shards(tokens, cotangent, selected, buckets, projector, intercepts, combiner, offset, relative, stretch, uplift,
           expander, threshold, reducer, residue, amplify, displace):
    quarter, width = tokens.shape
    cols = projector.shape[2]
    part = projector.shape[1]
    n, group = lax.axis_size("dp"), lax.axis_size("tensor")
    classes = relative.shape[0]
    length = group * quarter
    heads = cols // HEAD_DIM
    hidden = expander.shape[1]
    keep = -(-(quarter * 2 // 5) // 16) * 16
    lines = classes // group // n
    span = buckets.shape[0] + 1
    S, V = jax.ShapeDtypeStruct, pltpu.VMEM
    row = width // n
    ins = dict(tokens=tokens, cotangent=cotangent, selected=selected,
               buckets=jnp.pad(buckets, (1, 0), constant_values=-1).reshape(span // BLK, BLK),
               projector=projector, intercepts=intercepts, combiner=combiner, offset=offset, relative=relative, stretch=stretch, uplift=uplift,
               expander=expander, threshold=threshold, reducer=reducer, residue=residue, amplify=amplify, displace=displace)
    outs = dict(result=S((quarter, width), BF16), d_tokens=S((quarter, width), F32), weights=S((part, width), F32), sums=S((8, width), F32),
                rel_all=S((group, n, lines, width), BF16), exp_all=S((n, row, width), BF16), red_all=S((n, row, width), BF16))
    quarters, fews = (group, quarter, width), (group, keep, width)
    scratch = dict(
        own=V((part, width), BF16), pick=V((8, quarter), F32), x=V(quarters, BF16), w=V((n, part, width), BF16), chosen=V((group, 8, quarter), F32),
        sel=V((group, keep, quarter), BF16), probs=V((heads, length, length), F32), mixed=V((length, 3 * cols), BF16), table=V((span, 2 * cols), BF16),
        spread=V((span, classes), BF16), ctx=V((length, cols), BF16), far=V((length, length), F32), acc=V((length, cols), F32),
        part=V(quarters, BF16), part_slots=V((3, quarter, width), BF16), hidden=V(quarters, BF16), mid=V((quarter, width), F32), unit=V((quarter, width), F32),
        inverse=V((quarter, BLK), F32), feed=V(quarters, BF16), feed_slots=V((3, quarter, width), BF16), d_end=V((quarter, width), F32),
        d_rows=V(fews, BF16), small=V((8, width), F32), back=V(fews, BF16), back_slots=V((3, keep, width), BF16), d_mid=V((quarter, width), F32),
        d_attn=V(fews, BF16), d_exp=V((n, row, width), BF16), d_red=V((n, row, width), BF16), exp_slots=V((2, n // 2, row, width), BF16),
        red_slots=V((2, n // 2, row, width), BF16), dctx=V((length, cols), BF16), dctx_t=V((cols, length), BF16), turn_t=V((2 * cols, length), BF16),
        dq=V((length, cols), F32), dk=V((length, cols), F32), dv_t=V((cols, length), F32), dpos_t=V((2 * cols, span), F32), ds=V((length, length), BF16),
        grads=V((n, part, width), BF16), in_part=V(quarters, BF16), rel_part=V((group, classes // group, width), BF16),
        grad_slots=V((2, n // 2, part, width), BF16), in_slots=V((3, quarter, width), BF16), rel_slots=V((3, classes // group, width), BF16),
        rel_own=V((n, lines, width), BF16), rel_ring=V((2, n // 2, lines, width), BF16), small_all=V((n, 8, width), F32), small_slots=V((3, 8, width), F32),
        send=pltpu.SemaphoreType.DMA((11 * n + 40,)), recv=pltpu.SemaphoreType.DMA((11 * n + 40,)))
    made = pl.pallas_call(
        functools.partial(layer_kernel, n, list(ins) + list(outs) + list(scratch)),
        out_shape=tuple(outs.values()),
        scratch_shapes=list(scratch.values()),
        compiler_params=pltpu.CompilerParams(collective_id=1, has_side_effects=True),
        name="layer",
    )(*ins.values())
    kept = dict(zip(outs, made))
    kept["rel_all"] = kept["rel_all"].reshape(classes, width)
    kept["exp_all"] = kept["exp_all"].reshape(expander.shape)
    kept["red_all"] = kept["red_all"].reshape(reducer.shape)
    lasts = dict(out=S((quarter, width), BF16), tokens_grad=S((quarter, width), F32), projector_grad=S(projector.shape, F32),
                 intercepts_grad=S(intercepts.shape, F32), combiner_grad=S(combiner.shape, F32), offset_grad=S(offset.shape, F32),
                 relative_grad=S(relative.shape, F32), stretch_grad=S(stretch.shape, F32), uplift_grad=S(uplift.shape, F32),
                 expander_grad=S(expander.shape, F32), threshold_grad=S(threshold.shape, F32), reducer_grad=S(reducer.shape, F32),
                 residue_grad=S(residue.shape, F32), amplify_grad=S(amplify.shape, F32), displace_grad=S(displace.shape, F32))
    return pl.pallas_call(functools.partial(last_kernel, list(kept) + list(lasts)), out_shape=tuple(lasts.values()), name="last")(*kept.values())


def solution(mesh):
    both = P(("dp", "tensor"), None)
    return jax.shard_map(
        shards,
        mesh=mesh,
        in_specs=(both, both, P(("dp", "tensor")), P(), P(None, "dp", "tensor"), P(None, "tensor"), P("dp", "tensor"), P(), P(), P(), P(),
                  P(None, "tensor"), P("tensor"), P("tensor", None), P(), P(), P()),
        out_specs=(both, both, P(None, "dp", "tensor"), P(None, "tensor"), P("dp", "tensor"), P(), P(), P(), P(),
                   P(None, "tensor"), P("tensor"), P("tensor", None), P(), P(), P()),
        check_vma=False,
    )
```

time: 543 us -> 166 us (0.31)
  waiting for transfers between devices: 350 us -> 0 us
  Pallas kernels: 35.7 us -> 164 us
  blocking collectives: 96 us -> 0 us
  other arithmetic: 23 us -> 0 us
  matrix products: 14.6 us -> 0 us
  between operations: 14.6 us -> 0.83 us
  local copies, waits for them, and re-layouts: 8.64 us -> 1.35 us
    psum x2 -> x0, waiting for transfers between devices: 174 us -> none  [the longest x1 109 us: shards(): expander_grad, reducer_grad = lax.psum((expander_part, reducer_part), 'dp')]
    reduce_scatter x5 -> x0, waiting for transfers between devices: 144 us -> none  [the longest x1 66.4 us: shards(): lax.psum_scatter(grads, 'dp', scatter_dimension=0, tiled=True).astype(F32)]
    pallas_call x2, Pallas kernels: 35.7 us -> 164 us  [the longest x1 158 us: shards(): pl.pallas_call(functools.partial(layer_kernel, n, list(ins) + list(outs)...]
    psum x2 -> x0, blocking collectives: 59.5 us -> none  [the longest x1 37.1 us: shards(): small = lax.psum(small, ('dp', 'tensor'))]
    all_gather x5 -> x0, blocking collectives: 36.5 us -> none  [the longest x1 10.5 us: shards(): x = lax.all_gather(tokens, 'tensor', axis=0, tiled=True)]
    all_gather x1 -> x0, waiting for transfers between devices: 30.9 us -> none  [shards(): w = lax.all_gather(packed, 'dp', axis=0, tiled=True)]
    dot_general x10 -> x0, matrix products: 14.6 us -> none  [the longest x3 6.02 us: tn(): lax.dot_general(a, b, (((0,), (0,)), ((), ())), preferred_element_type=F32)]
    convert_element_type x10 -> x0, other arithmetic: 10.4 us -> none  [the longest x1 2.94 us: shards(): expander_grad.astype(F32)]
  transfers between devices with their start and end apart: 8 -> 0, of which waited for: 8 -> 0; matrix products, arithmetic and copies ran while one was open for 4% -> 0% of each run, Pallas kernels for 0% -> 0%
where the time goes in v3:
time: 166 us
  Pallas kernels  164 us (99%)
    pallas_call x1, Pallas kernels, shards(): pl.pallas_call(functools.partial(layer_kernel, n, list(ins) + list(outs)...  158 us
    pallas_call x1, Pallas kernels, shards(): pl.pallas_call(functools.partial(last_kernel, list(kept) + list(lasts)),...  5.29 us

profile of v3, /device:TPU:0, one launch (start us, length us, event | category | flops | bytes accessed | tf_op | source)
XLA Modules:
  0.0 165.9 jit_solution(11917463295083970871)
XLA Ops:
  0.6 1.4 pad_bitcast_fusion.refs_3_
  2.0 158.4 %layer.1 = (bf16[128,768]{1,0:T(8,128)(2,1)}, f32[128,768]{1,0:T(8,128)}, f32[96,768]{1,0:T(8,128)}, f32[8,768]{1,0:T(8,128)}, bf16[4,8,16,768]{3,2,1,0:T(8,128)...) custom-call(bf16[128,768]{1,0:T(8,128)(2,1)} %refs_0_.1, bf16[128,768]{1,0:T(8,128)(2,1)} %refs_1_.1, ...), custom_call_target="tpu_custom_call" | custom-call | tf_op jit(solution)/shard_map/layer/pallas_call | solution.py:563
  160.4 5.3 %last.1 = (bf16[128,768]{1,0:T(8,128)(2,1)}, f32[128,768]{1,0:T(8,128)}, f32[3,96,192]{2,1,0:T(8,128)}, f32[3,192]{1,0:T(4,128)}, f32[96,192]{1,0:T(8,128)}, /*i...) custom-call(bf16[128,768]{1,0:T(8,128)(2,1)} %get-tuple-element.22.r, ...), custom_call_target="tpu_custom_call" | custom-call | tf_op jit(solution)/shard_map/last/pallas_call | solution.py:579
